TPU v7x, 512 devices: a whole 4x8x8 slice. The times are simulated.
512 devices in a mesh: gx: 64 (over z, y_hi, x), gy: 8 (over y_lo, core).
Axes of the slice: x: 4, y: 8 (y_hi: 2, y_lo: 4; y = y_hi * 4 + y_lo), z: 8, core: 2. Of those that a mesh axis runs over, the one named last changes fastest.
Arguments:
- offsets: float32 [3, 64, 64, 512], P(None, 'gx', 'gy'), may hold values from 0 to 1
- masses: float32 [64, 64, 512], P('gx', 'gy'), may hold values from 0.02 to 0.2
- kernel: bfloat16 [36, 2, 36, 64, 4096], P(None, None, None, 'gx', 'gy'), may hold values from -1.2 to 3.2, as said below
Outputs:
- acceleration: float32 [3, 64, 64, 512], P(None, 'gx', 'gy')
Inputs may be any that keep to these rules, and one draw needn't show every extreme that they name: `kernel`: G is Hermitian in the wavevector: the entry at -k (each component modulo the grid) is the complex conjugate of the entry at k; all entries at the zero wavevector are zero.
All inputs are finite; a program needn't handle non-finite values.
Results may differ from a plain program's by a relative error of at most 0.0003.
Values sent between devices are 32-bit elements; how exact they have to be, the bound alone decides.
No kernel may reach another device: no remote copies, remote signals or barrier semaphores. Data moves between devices by JAX's collectives and lax.ppermute only.
A program may use at most 128 MiB of HBM per device.

v0:
```python
import math

import jax
import jax.numpy as jnp
from jax import lax
from jax.sharding import PartitionSpec as P

BODIES = 8


SOFTEN = 0.5


def extended_2(cells, sides, width):
    for axis, dim in sides:
        count = lax.axis_size(axis)
        head = lax.slice_in_dim(cells, 0, width, axis=dim)
        tail = lax.slice_in_dim(cells, cells.shape[dim] - width, cells.shape[dim], axis=dim)
        cells = jnp.concatenate(
            [
                lax.ppermute(tail, axis, [(i, (i + 1) % count) for i in range(count)]),
                cells,
                lax.ppermute(head, axis, [((i + 1) % count, i) for i in range(count)]),
            ],
            axis=dim,
        )
    return cells


def channel_list():
    listed = []
    for pow_z in range(2):
        for pow_x in range(6 - pow_z):
            for pow_y in range(6 - pow_z - pow_x):
                listed.append((pow_x, pow_y, pow_z))
    return listed


def powers(values, highest):
    result = [jnp.ones_like(values)]
    for degree in range(highest):
        result.append(result[-1] * values)
    return result


def contract(form, left, right):
    return jnp.einsum(
        form, left, right, precision=lax.Precision.HIGHEST, preferred_element_type=jnp.float32
    )


def dft_tables(length):
    counter = jnp.arange(length, dtype=jnp.int32)
    product = counter[:, None] * counter[None, :] % length
    angle = product.astype(jnp.float32) * (2.0 * math.pi / length)
    return (jnp.cos(angle), jnp.sin(angle))


def far_accel(local_field, along_x, along_y, along_z):
    accel = [jnp.zeros_like(along_x[1]) for axis_index in range(3)]
    for chan_index, (pow_x, pow_y, pow_z) in enumerate(channel_list()):
        coefficient = local_field[chan_index][:, :, None, :]
        if pow_x > 0:
            accel[0] = accel[0] - coefficient * (
                pow_x * along_x[pow_x - 1] * along_y[pow_y] * along_z[pow_z]
            )
        if pow_y > 0:
            accel[1] = accel[1] - coefficient * (
                pow_y * along_x[pow_x] * along_y[pow_y - 1] * along_z[pow_z]
            )
        if pow_z > 0:
            accel[2] = accel[2] - coefficient * (along_x[pow_x] * along_y[pow_y])
    return jnp.stack(accel)


def y_forward(pieces):
    cos_table, sin_table = dft_tables(pieces.shape[3])
    out_real = contract("cxnz,nk->cxkz", pieces[0], cos_table) + contract(
        "cxnz,nk->cxkz", pieces[1], sin_table
    )
    out_imag = contract("cxnz,nk->cxkz", pieces[1], cos_table) - contract(
        "cxnz,nk->cxkz", pieces[0], sin_table
    )
    return jnp.stack([out_real, out_imag])


def x_forward(pieces):
    cos_table, sin_table = dft_tables(pieces.shape[2])
    out_real = contract("cnyz,nk->cyzk", pieces[0], cos_table) + contract(
        "cnyz,nk->cyzk", pieces[1], sin_table
    )
    out_imag = contract("cnyz,nk->cyzk", pieces[1], cos_table) - contract(
        "cnyz,nk->cyzk", pieces[0], sin_table
    )
    return jnp.stack([out_real, out_imag])


def y_inverse(pieces):
    cos_table, sin_table = dft_tables(pieces.shape[3])
    out_real = contract("cxkz,kn->cxnz", pieces[0], cos_table) - contract(
        "cxkz,kn->cxnz", pieces[1], sin_table
    )
    out_imag = contract("cxkz,kn->cxnz", pieces[1], cos_table) + contract(
        "cxkz,kn->cxnz", pieces[0], sin_table
    )
    return jnp.stack([out_real, out_imag])


def z_inverse(pieces):
    cos_table, sin_table = dft_tables(pieces.shape[4])
    out_real = contract("cxyk,kn->cxyn", pieces[0], cos_table) - contract(
        "cxyk,kn->cxyn", pieces[1], sin_table
    )
    out_imag = contract("cxyk,kn->cxyn", pieces[1], cos_table) + contract(
        "cxyk,kn->cxyn", pieces[0], sin_table
    )
    return jnp.stack([out_real, out_imag])


def inverse_pass(local_real, local_imag, total_x):
    chan_count = local_real.shape[0]
    rows_k = local_real.shape[1]
    planes_k = local_real.shape[2] // total_x
    spec_real = local_real.reshape(chan_count, rows_k, planes_k, total_x)
    spec_imag = local_imag.reshape(chan_count, rows_k, planes_k, total_x)
    cos_table, sin_table = dft_tables(total_x)
    along_real = contract("cyzk,kn->cnyz", spec_real, cos_table) - contract(
        "cyzk,kn->cnyz", spec_imag, sin_table
    )
    along_imag = contract("cyzk,kn->cnyz", spec_imag, cos_table) + contract(
        "cyzk,kn->cnyz", spec_real, sin_table
    )
    stacked = jnp.stack([along_real, along_imag])
    lines_y = y_inverse(lax.all_to_all(stacked, "gx", split_axis=2, concat_axis=3, tiled=True))
    return z_inverse(lax.all_to_all(lines_y, "gy", split_axis=3, concat_axis=4, tiled=True))


def far_field(offsets, masses, kernel):
    planes_x = offsets.shape[1]
    rows_y = offsets.shape[2]
    cells_z = offsets.shape[3] // BODIES
    total_x = planes_x * lax.axis_size("gx")
    total_y = rows_y * lax.axis_size("gy")
    body_pos = offsets.reshape(3, planes_x, rows_y, BODIES, cells_z)
    mass_cells = masses.reshape(planes_x, rows_y, BODIES, cells_z)
    scaled = 2.0 * body_pos - 1.0
    along_x = powers(scaled[0], 5)
    along_y = powers(scaled[1], 5)
    along_z = powers(scaled[2], 1)
    listed = channel_list()
    chan_count = len(listed)
    moments = jnp.stack(
        [
            jnp.sum(mass_cells * (along_x[pow_x] * along_y[pow_y] * along_z[pow_z]), axis=2)
            for pow_x, pow_y, pow_z in listed
        ]
    )
    cos_table, sin_table = dft_tables(cells_z)
    first_real = contract("cxyn,nk->cxyk", moments, cos_table)
    first_imag = -contract("cxyn,nk->cxyk", moments, sin_table)
    stacked = jnp.stack([first_real, first_imag])
    lines_y = y_forward(lax.all_to_all(stacked, "gy", split_axis=4, concat_axis=3, tiled=True))
    spectrum = x_forward(lax.all_to_all(lines_y, "gx", split_axis=3, concat_axis=2, tiled=True))
    rows_k = spectrum.shape[2]
    spec_real = spectrum[0].reshape(chan_count, rows_k, -1)
    spec_imag = spectrum[1].reshape(chan_count, rows_k, -1)
    gain_real = kernel[:, 0]
    gain_imag = kernel[:, 1]
    local_real = contract("dcyk,cyk->dyk", gain_real, spec_real) - contract(
        "dcyk,cyk->dyk", gain_imag, spec_imag
    )
    local_imag = contract("dcyk,cyk->dyk", gain_real, spec_imag) + contract(
        "dcyk,cyk->dyk", gain_imag, spec_real
    )
    inv_count = 1.0 / (total_x * total_y * cells_z)
    paired = inverse_pass(
        local_real[0::2] - local_imag[1::2], local_imag[0::2] + local_real[1::2], total_x
    )
    local_field = (
        jnp.stack([paired[0], paired[1]], axis=1).reshape(chan_count, planes_x, rows_y, cells_z)
        * inv_count
    )
    return far_accel(local_field, along_x, along_y, along_z)


def near_field(offsets, masses):
    planes_x = offsets.shape[1]
    rows_y = offsets.shape[2]
    row_width = offsets.shape[3]
    cells_z = row_width // BODIES
    packed_bodies = jnp.concatenate([offsets, masses[None]], axis=0)
    extended = extended_2(packed_bodies, (("gx", 1), ("gy", 2)), 1)
    own_pos = offsets.reshape(3, planes_x, rows_y, BODIES, cells_z)
    target = jnp.tile(own_pos, (1, 1, 1, 1, BODIES))
    summed = jnp.zeros(target.shape, jnp.float32)
    for shift_x in (-1, 0, 1):
        for shift_y in (-1, 0, 1):
            window_cells = extended[
                :, 1 + shift_x : 1 + shift_x + planes_x, 1 + shift_y : 1 + shift_y + rows_y
            ]
            window_cells = window_cells.reshape(4, planes_x, rows_y, BODIES, cells_z)
            for shift_z in (-1, 0, 1):
                neighbour = jnp.roll(window_cells, -shift_z, axis=4).reshape(
                    4, planes_x, rows_y, 1, row_width
                )
                offset_vec = jnp.array([shift_x, shift_y, shift_z], jnp.float32).reshape(
                    3, 1, 1, 1, 1
                )
                separation = neighbour[:3] + offset_vec - target
                distance_sq = jnp.sum(separation * separation, axis=0) + SOFTEN * SOFTEN
                inverse_r = lax.rsqrt(distance_sq)
                summed = summed + separation * (neighbour[3] * inverse_r * inverse_r * inverse_r)
    summed = summed.reshape(3, planes_x, rows_y, BODIES, BODIES, cells_z).sum(axis=4)
    return summed


def local(offsets, masses, kernel):
    planes_x = offsets.shape[1]
    rows_y = offsets.shape[2]
    row_width = offsets.shape[3]
    far_part = far_field(offsets, masses, kernel)
    near_part = near_field(offsets, masses)
    return (far_part + near_part).reshape(3, planes_x, rows_y, row_width)


def solution(mesh):
    placed = (P(None, "gx", "gy", None), P("gx", "gy", None), P(None, None, None, "gx", "gy"))
    return jax.shard_map(
        local, mesh=mesh, in_specs=placed, out_specs=P(None, "gx", "gy", None), check_vma=False
    )
```

profile of v0, /device:TPU:1, one launch (start us, length us, event | category | flops | bytes accessed | tf_op | source)
XLA Modules:
  0.0 197.6 jit_solution(1248578561568946406)
XLA Ops:
  0.0 1.5 pad_maximum_fusion.6
  1.5 18.9 %collective-permute-start.1 = (f32[4,1,8,512]{3,2,1,0:T(8,128)}, f32[4,1,8,512]{3,2,1,0:T(8,128)S(1)}, u32[]{:S(2)}, u32[]{:S(2)}) collective-permute-start(f32[4,1,8,512]{3,2,1,0:T(8,128)} %pad_maximum_fusion.6), channel_id=1, source_target_pairs={{8,0},{16,8},{24,16},{32,24},{40,32},{48,40},{56,48},{64,56},{72,6... | collective-permute-start | bytes 196616 | tf_op jit(solution)/shard_map/ppermute | solution.py:23
  20.4 1.9 collective-permute-start
  27.6 2.3 %reshape.4054 = f32[8,1,4608]{2,1,0:T(1,128)} reshape(f32[64,2,1,8,36]{4,3,2,1,0:T(8,128)} %bitcast.694) | data formatting | bytes 294912
  29.8 4.8 %all-to-all-start = ((f32[8,1,4608]{2,1,0:T(1,128)}), f32[8,1,4608]{2,1,0:T(1,128)}, u32[]{:S(2)}, u32[]{:S(2)}) async-start(f32[8,1,4608]{2,1,0:T(1,128)} %reshape.4054), calls=%async_computation | async-start | bytes 294912 | tf_op jit(solution)/shard_map/all_to_all | solution.py:162
  35.9 6.0 %fusion.416 = (bf16[36,1,36,1,512]{4,1,3,2,0:T(2,128)(2,1)}, bf16[36,1,36,1,512]{4,1,3,2,0:T(2,128)(2,1)}) fusion(bf16[36,2,36,1,512]{4,1,3,2,0:T(2,128)(2,1)S(1)} %copy-done), kind=kLoop, calls=%fused_computation.654 | loop fusion | bytes 5308416 | tf_op jit(solution)/shard_map/slice | solution.py:168
  44.0 2.1 %collective-permute-start.3 = (f32[4,3,1,512]{3,2,1,0:T(1,128)S(1)}, f32[4,3,1,512]{3,2,1,0:T(1,128)S(1)}, u32[]{:S(2)}, u32[]{:S(2)}) collective-permute-start(f32[4,3,1,512]{3,2,1,0:T(1,128)S(1)} %get-tuple-element.103), channel_id=1, source_target_pairs={{1,0},{2,1},{3,2},{4,3},{5,4},{6,5},{7,6},{0,7},{9,8},{10,9},{11,1... | collective-permute-start | bytes 73736 | tf_op jit(solution)/shard_map/ppermute | solution.py:23
  46.0 3.7 %collective-permute-start.2 = (f32[4,3,1,512]{3,2,1,0:T(1,128)S(1)}, f32[4,3,1,512]{3,2,1,0:T(1,128)S(1)}, u32[]{:S(2)}, u32[]{:S(2)}) collective-permute-start(f32[4,3,1,512]{3,2,1,0:T(1,128)S(1)} %get-tuple-element.104), channel_id=1, source_target_pairs={{0,1},{1,2},{2,3},{3,4},{4,5},{5,6},{6,7},{7,0},{8,9},{9,10},{10,1... | collective-permute-start | bytes 73736 | tf_op jit(solution)/shard_map/ppermute | solution.py:21
  62.5 1.4 pad_maximum_fusion.8
  63.8 1.5 slice.732
  70.2 1.5 slice.694
  77.6 2.9 %multiply_reduce_fusion.26 = (f32[8,8,8,64]{3,2,1,0:T(8,128)S(1)}, f32[8,8,8,64]{3,2,1,0:T(8,128)S(1)}, f32[8,8,8,64]{3,2,1,0:T(8,128)S(1)}, f32[8,8,8,64]{3,2,1...) fusion(f32[3,8,8,64]{3,2,1,0:T(8,128)S(1)} %tile.10, ...), kind=kLoop, calls=%fused_computation.54 | loop fusion | flops 4980736 | bytes 3424256 | tf_op jit(solution)/shard_map/reduce_sum | solution.py:210
  101.6 1.9 reduce.99
  107.9 12.1 %all-to-all-start.1 = ((f32[64,1,576]{2,1,0:T(1,128)}), f32[64,1,576]{2,1,0:T(1,128)S(1)}, u32[]{:S(2)}, u32[]{:S(2)}) async-start(f32[64,1,576]{2,1,0:T(1,128)} %reshape.4056), calls=%async_computation.1 | async-start | bytes 327680 | tf_op jit(solution)/shard_map/all_to_all | solution.py:163
  121.6 12.1 %all-to-all-done.1 = f32[64,1,576]{2,1,0:T(1,128)S(1)} async-done(((f32[64,1,576]{2,1,0:T(1,128)}), f32[64,1,576]{2,1,0:T(1,128)S(1)}, u32[]{:S(2)}, u32[]{:S(2)}) %all-to-all-start.1) | async-done | bytes 147488 | tf_op jit(solution)/shard_map/all_to_all | solution.py:163
  133.7 1.7 reduce.100
  135.4 1.4 reshape.4057
  141.9 3.9 %fusion = (f32[512,36]{0,1:T(8,128)S(1)}, f32[512,36]{0,1:T(8,128)S(1)}, f32[512,36]{0,1:T(8,128)S(1)}, f32[512,36]{0,1:T(8,128)S(1)}) fusion(f32[512,36]{0,1:T(8,128)S(1)} %bitcast.710, bf16[36,1,36,1,512]{4,1,3,2,0:T(2,128)(2,1)} %get-tuple-element.74, f32[512,36]{0,1:T(8,128)S(1)} %bitcast.711, bf16[36,1,36,1,512]{4,1,3,2,0:T(2,128)(2,1)S(1)} %copy-done.1), kind=kLoop, calls=%fused_computation.4 | loop fusion | flops 6561792 | bytes 3096576 | tf_op jit(solution)/shard_map/dcyk,cyk->dyk/dot_general | solution.py:47
  149.0 4.7 %all-to-all-start.2 = ((f32[64,1,288]{2,1,0:T(1,128)}), f32[64,1,288]{2,1,0:T(1,128)S(1)}, u32[]{:S(2)}, u32[]{:S(2)}) async-start(f32[64,1,288]{2,1,0:T(1,128)} %reshape.4058), calls=%async_computation.2 | async-start | bytes 196608 | tf_op jit(solution)/shard_map/all_to_all | solution.py:134
  154.5 12.6 %all-to-all-done.2 = f32[64,1,288]{2,1,0:T(1,128)S(1)} async-done(((f32[64,1,288]{2,1,0:T(1,128)}), f32[64,1,288]{2,1,0:T(1,128)S(1)}, u32[]{:S(2)}, u32[]{:S(2)}) %all-to-all-start.2) | async-done | bytes 73760 | tf_op jit(solution)/shard_map/all_to_all | solution.py:134
  167.1 1.5 reduce.101
  168.7 1.4 reshape.4059
  177.6 9.4 %all-to-all-start.3 = ((f32[8,1,2304]{2,1,0:T(1,128)}), f32[8,1,2304]{2,1,0:T(1,128)S(1)}, u32[]{:S(2)}, u32[]{:S(2)}) async-start(f32[8,1,2304]{2,1,0:T(1,128)} %reshape.4060), calls=%async_computation.3 | async-start | bytes 147456 | tf_op jit(solution)/shard_map/all_to_all | solution.py:135
  187.0 5.4 %add_reduce_fusion = f32[3,8,8,64]{3,2,1,0:T(8,128)S(1)} fusion(f32[8,8,8,64]{3,2,1,0:T(8,128)S(1)} %copy-done.12, f32[3,8,8,64]{3,2,1,0:T(8,128)} %copy-done.15, f32[8,8,8,64]{3,2,1,0:T(8,128)S(1)} %copy-done.11, f32[3,8,8,64]{3,2,1,0:T(8,128)} %copy-done.18, f32[8,8,8,64]{3,2,1,0:T(8,128)S(1)} %copy-done.10, f32[3,8,8,64]{3,2,1,0:T(8,128)} %copy-done.17, ...), kind=kLoop, calls=%fused_computation.27 | loop fusion | flops 7950336 | bytes 4915200 | tf_op jit(solution)/shard_map/reduce_sum | solution.py:213
  (374 shorter events, 79.3 us)
Async XLA Ops:
  0.0 34.7 %copy-start.2 = (f32[3,1,8,512]{3,2,1,0:T(8,128)S(1)}, f32[3,1,8,512]{3,2,1,0:T(8,128)}, u32[]{:S(2)}) copy-start(f32[3,1,8,512]{3,2,1,0:T(8,128)} %param.30) | copy-start | bytes 147460
  0.0 34.7 %copy-start.3 = (f32[1,8,512]{2,1,0:T(8,128)S(1)}, f32[1,8,512]{2,1,0:T(8,128)}, u32[]{:S(2)}) copy-start(f32[1,8,512]{2,1,0:T(8,128)} %param.31) | copy-start | bytes 49156
  1.5 41.8 %collective-permute-start.1 = (f32[4,1,8,512]{3,2,1,0:T(8,128)}, f32[4,1,8,512]{3,2,1,0:T(8,128)S(1)}, u32[]{:S(2)}, u32[]{:S(2)}) collective-permute-start(f32[4,1,8,512]{3,2,1,0:T(8,128)} %pad_maximum_fusion.6), channel_id=1, source_target_pairs={{8,0},{16,8},{24,16},{32,24},{40,32},{48,40},{56,48},{64,56},{72,6... | collective-permute-start | bytes 196616 | tf_op jit(solution)/shard_map/ppermute | solution.py:23
  20.4 23.2 %collective-permute-start = (f32[4,1,8,512]{3,2,1,0:T(8,128)}, f32[4,1,8,512]{3,2,1,0:T(8,128)S(1)}, u32[]{:S(2)}, u32[]{:S(2)}) collective-permute-start(f32[4,1,8,512]{3,2,1,0:T(8,128)} %pad_maximum_fusion.6), channel_id=1, source_target_pairs={{0,8},{8,16},{16,24},{24,32},{32,40},{40,48},{48,56},{56,64},{64,7... | collective-permute-start | bytes 196616 | tf_op jit(solution)/shard_map/ppermute | solution.py:21
  29.8 71.2 %all-to-all-start = ((f32[8,1,4608]{2,1,0:T(1,128)}), f32[8,1,4608]{2,1,0:T(1,128)}, u32[]{:S(2)}, u32[]{:S(2)}) async-start(f32[8,1,4608]{2,1,0:T(1,128)} %reshape.4054), calls=%async_computation | async-start | bytes 294912 | tf_op jit(solution)/shard_map/all_to_all | solution.py:162
  42.6 34.8 %copy-start.36 = (f32[3,8,8,64]{3,2,1,0:T(8,128)}, f32[3,8,8,64]{3,2,1,0:T(8,128)S(1)}, u32[]{:S(2)}) copy-start(f32[3,8,8,64]{3,2,1,0:T(8,128)S(1)} %get-tuple-element.223) | copy-start | bytes 147460
  44.0 8.8 %collective-permute-start.3 = (f32[4,3,1,512]{3,2,1,0:T(1,128)S(1)}, f32[4,3,1,512]{3,2,1,0:T(1,128)S(1)}, u32[]{:S(2)}, u32[]{:S(2)}) collective-permute-start(f32[4,3,1,512]{3,2,1,0:T(1,128)S(1)} %get-tuple-element.103), channel_id=1, source_target_pairs={{1,0},{2,1},{3,2},{4,3},{5,4},{6,5},{7,6},{0,7},{9,8},{10,9},{11,1... | collective-permute-start | bytes 73736 | tf_op jit(solution)/shard_map/ppermute | solution.py:23
  46.0 6.8 %collective-permute-start.2 = (f32[4,3,1,512]{3,2,1,0:T(1,128)S(1)}, f32[4,3,1,512]{3,2,1,0:T(1,128)S(1)}, u32[]{:S(2)}, u32[]{:S(2)}) collective-permute-start(f32[4,3,1,512]{3,2,1,0:T(1,128)S(1)} %get-tuple-element.104), channel_id=1, source_target_pairs={{0,1},{1,2},{2,3},{3,4},{4,5},{5,6},{6,7},{7,0},{8,9},{9,10},{10,1... | collective-permute-start | bytes 73736 | tf_op jit(solution)/shard_map/ppermute | solution.py:21
  55.3 22.1 %copy-start.25 = (f32[3,8,8,64]{3,2,1,0:T(8,128)}, f32[3,8,8,64]{3,2,1,0:T(8,128)S(1)}, u32[]{:S(2)}) copy-start(f32[3,8,8,64]{3,2,1,0:T(8,128)S(1)} %fusion.91) | copy-start | bytes 147460
  56.7 24.9 %copy-start.15 = (f32[3,8,8,64]{3,2,1,0:T(8,128)}, f32[3,8,8,64]{3,2,1,0:T(8,128)S(1)}, u32[]{:S(2)}) copy-start(f32[3,8,8,64]{3,2,1,0:T(8,128)S(1)} %fusion.43) | copy-start | bytes 147460
  57.7 17.7 %copy-start.78 = (f32[3]{0:T(128)S(1)}, f32[3]{0:T(128)}, u32[]{:S(2)}) copy-start(f32[3]{0:T(128)} %constant.113.clone) | copy-start | bytes 40
  107.9 25.8 %all-to-all-start.1 = ((f32[64,1,576]{2,1,0:T(1,128)}), f32[64,1,576]{2,1,0:T(1,128)S(1)}, u32[]{:S(2)}, u32[]{:S(2)}) async-start(f32[64,1,576]{2,1,0:T(1,128)} %reshape.4056), calls=%async_computation.1 | async-start | bytes 327680 | tf_op jit(solution)/shard_map/all_to_all | solution.py:163
  149.0 18.1 %all-to-all-start.2 = ((f32[64,1,288]{2,1,0:T(1,128)}), f32[64,1,288]{2,1,0:T(1,128)S(1)}, u32[]{:S(2)}, u32[]{:S(2)}) async-start(f32[64,1,288]{2,1,0:T(1,128)} %reshape.4058), calls=%async_computation.2 | async-start | bytes 196608 | tf_op jit(solution)/shard_map/all_to_all | solution.py:134
  168.6 18.4 %copy-start.4 = (f32[8,8,8,64]{3,2,1,0:T(8,128)S(1)}, f32[8,8,8,64]{3,2,1,0:T(8,128)}, u32[]{:S(2)}) copy-start(f32[8,8,8,64]{3,2,1,0:T(8,128)} %multiply_multiply_fusion.13) | copy-start | bytes 393220
  168.6 18.4 %copy-start.5 = (f32[8,8,8,64]{3,2,1,0:T(8,128)S(1)}, f32[8,8,8,64]{3,2,1,0:T(8,128)}, u32[]{:S(2)}) copy-start(f32[8,8,8,64]{3,2,1,0:T(8,128)} %multiply_multiply_fusion.25) | copy-start | bytes 393220
  168.6 18.4 %copy-start.6 = (f32[8,8,8,64]{3,2,1,0:T(8,128)S(1)}, f32[8,8,8,64]{3,2,1,0:T(8,128)}, u32[]{:S(2)}) copy-start(f32[8,8,8,64]{3,2,1,0:T(8,128)} %multiply_multiply_fusion.6) | copy-start | bytes 393220
  168.6 18.4 %copy-start.7 = (f32[8,8,8,64]{3,2,1,0:T(8,128)S(1)}, f32[8,8,8,64]{3,2,1,0:T(8,128)}, u32[]{:S(2)}) copy-start(f32[8,8,8,64]{3,2,1,0:T(8,128)} %multiply_multiply_fusion.5) | copy-start | bytes 393220
  168.6 18.4 %copy-start.8 = (f32[8,8,8,64]{3,2,1,0:T(8,128)S(1)}, f32[8,8,8,64]{3,2,1,0:T(8,128)}, u32[]{:S(2)}) copy-start(f32[8,8,8,64]{3,2,1,0:T(8,128)} %multiply_multiply_fusion.4) | copy-start | bytes 393220
  168.6 18.4 %copy-start.9 = (f32[8,8,8,64]{3,2,1,0:T(8,128)S(1)}, f32[8,8,8,64]{3,2,1,0:T(8,128)}, u32[]{:S(2)}) copy-start(f32[8,8,8,64]{3,2,1,0:T(8,128)} %multiply_multiply_fusion.3) | copy-start | bytes 393220
  168.6 18.4 %copy-start.10 = (f32[8,8,8,64]{3,2,1,0:T(8,128)S(1)}, f32[8,8,8,64]{3,2,1,0:T(8,128)}, u32[]{:S(2)}) copy-start(f32[8,8,8,64]{3,2,1,0:T(8,128)} %multiply_multiply_fusion.2) | copy-start | bytes 393220
  168.6 18.4 %copy-start.11 = (f32[8,8,8,64]{3,2,1,0:T(8,128)S(1)}, f32[8,8,8,64]{3,2,1,0:T(8,128)}, u32[]{:S(2)}) copy-start(f32[8,8,8,64]{3,2,1,0:T(8,128)} %multiply_multiply_fusion.1) | copy-start | bytes 393220
  168.6 18.4 %copy-start.12 = (f32[8,8,8,64]{3,2,1,0:T(8,128)S(1)}, f32[8,8,8,64]{3,2,1,0:T(8,128)}, u32[]{:S(2)}) copy-start(f32[8,8,8,64]{3,2,1,0:T(8,128)} %multiply_multiply_fusion) | copy-start | bytes 393220
  168.6 18.4 %copy-start.13 = (f32[8,8,8,64]{3,2,1,0:T(8,128)S(1)}, f32[8,8,8,64]{3,2,1,0:T(8,128)}, u32[]{:S(2)}) copy-start(f32[8,8,8,64]{3,2,1,0:T(8,128)} %multiply_multiply_fusion.26) | copy-start | bytes 393220
  177.6 15.0 %all-to-all-start.3 = ((f32[8,1,2304]{2,1,0:T(1,128)}), f32[8,1,2304]{2,1,0:T(1,128)S(1)}, u32[]{:S(2)}, u32[]{:S(2)}) async-start(f32[8,1,2304]{2,1,0:T(1,128)} %reshape.4060), calls=%async_computation.3 | async-start | bytes 147456 | tf_op jit(solution)/shard_map/all_to_all | solution.py:135
  (69 other events, 364.2 us)
where the time goes:
time: 199 us; the launch traced here: 198 us
  other arithmetic  58.1 us (29%)
  starting transfers between devices  57.7 us (29%)
  local copies, waits for them, and re-layouts  45.8 us (23%)
  waiting for transfers between devices  24.7 us (12%)
  matrix products  9.58 us (5%)
    mul x43, other arithmetic, near_field(): neighbour[3] * inverse_r * inverse_r * inverse_r  25.3 us
    ppermute x2, starting transfers between devices, extended_2(): lax.ppermute(head, axis, [((i + 1) % count, i) for i in range(count)])  21 us
    unnamed x182, local copies, waits for them, and re-layouts  14.2 us
    all_to_all x1, waiting for transfers between devices, inverse_pass(): lax.all_to_all(stacked, 'gx', split_axis=2, concat_axis=3, tiled=True)  12.6 us
    all_to_all x1, starting transfers between devices, far_field(): lax.all_to_all(lines_y, 'gx', split_axis=3, concat_axis=2, tiled=True)  12.1 us
    all_to_all x1, waiting for transfers between devices, far_field(): lax.all_to_all(lines_y, 'gx', split_axis=3, concat_axis=2, tiled=True)  12.1 us
    dot_general x22, matrix products, contract(): jnp.einsum(form, left, right, precision=lax.Precision.HIGHEST, preferred_...  9.58 us
    all_to_all x1, starting transfers between devices, inverse_pass(): lax.all_to_all(lines_y, 'gy', split_axis=3, concat_axis=4, tiled=True)  9.38 us
  transfers between devices with their start and end apart: 8, of which 2 were waited for; matrix products, arithmetic and copies ran while one was open for 38% of the time, Pallas kernels for 0%

commit v1 on v0

v1 whole, which is shorter than its diff:
```python
import math

import jax
import jax.numpy as jnp
import numpy as np
from jax import lax
from jax.experimental import pallas as pl
from jax.experimental.pallas import tpu as pltpu
from jax.sharding import PartitionSpec as P

SOFTEN = 0.5
N = 64
KEEP = 5
GROUP = 2 * KEEP
MOMENTS = 36
LANES = 384
VMEM = pltpu.VMEM


def channel_list():
    listed = []
    for pow_z in range(2):
        for pow_x in range(6 - pow_z):
            for pow_y in range(6 - pow_z - pow_x):
                listed.append((pow_x, pow_y, pow_z))
    return listed


def split_np(table):
    high = np.asarray(table, np.float32).astype(jnp.bfloat16)
    low = (np.asarray(table, np.float64) - high.astype(np.float64)).astype(jnp.bfloat16)
    return high, low


def angles(rows, columns):
    product = np.outer(np.asarray(rows), np.asarray(columns)) % N
    return product * (2.0 * math.pi / N)


def kept_kz():
    return np.array([8 * block + offset for block in range(8) for offset in range(KEEP)])


def table_z_forward():
    angle = angles(np.arange(N), kept_kz()).reshape(N, 8, 1, KEEP)
    both = np.concatenate([np.cos(angle), -np.sin(angle)], axis=2).reshape(N, 8 * GROUP)
    both = np.pad(both, ((0, 0), (0, 128 - 8 * GROUP)))
    high, low = split_np(both)
    return np.concatenate([high, low, high, np.zeros_like(high)], axis=0)


def table_left():
    angle = angles(np.arange(N), np.arange(N))
    high, low = split_np(np.concatenate([np.cos(angle), np.sin(angle)], axis=0))
    return np.concatenate([high, low, high], axis=1)


def table_x_forward():
    angle = angles(np.arange(N), np.arange(N))
    high, low = split_np(np.concatenate([np.cos(angle), np.sin(angle)], axis=1))
    return np.concatenate([high, low, high, np.zeros_like(high)], axis=0)


def table_x_inverse():
    angle = angles(np.arange(N), np.arange(N))
    high, low = split_np(np.concatenate([np.cos(angle), np.sin(angle)], axis=1))
    return np.concatenate([high, low, high], axis=1)


def table_z_inverse():
    angle = angles(kept_kz(), np.arange(N)).reshape(8, 1, KEEP, N)
    weight = np.where(np.arange(KEEP) % 4 == 0, 1.0, 2.0).reshape(1, 1, KEEP, 1)
    both = np.concatenate([np.cos(angle), -np.sin(angle)], axis=1) * weight / float(N**3)
    both = np.pad(both.reshape(8 * GROUP, N), ((0, 128 - 8 * GROUP), (0, 0)))
    both = np.concatenate([both, both], axis=1)
    high, low = split_np(both)
    return np.concatenate([high, high, low], axis=0)


def split(value):
    high = value.astype(jnp.bfloat16)
    low = (value - high.astype(jnp.float32)).astype(jnp.bfloat16)
    return high, low


def mxu(left, right):
    return jnp.dot(left, right, preferred_element_type=jnp.float32)


def mxu_nt(left, right):
    return lax.dot_general(
        left, right, (((1,), (1,)), ((), ())), preferred_element_type=jnp.float32
    )


def powers(values, highest):
    result = [None, values]
    for _ in range(highest - 1):
        result.append(result[-1] * values)
    return result


def moments_kernel(offsets, masses, table, chunks, packed, moments):
    mass = masses[0]
    for comp in range(3):
        packed[comp] = offsets[comp, 0]
    packed[3] = mass
    along_x = powers(2.0 * offsets[0, 0] - 1.0, 5)
    along_y = powers(2.0 * offsets[1, 0] - 1.0, 5)
    along_z = 2.0 * offsets[2, 0] - 1.0
    channel = 0
    for pow_z in range(2):
        lead_z = mass * along_z if pow_z else mass
        for pow_x in range(6 - pow_z):
            lead = lead_z * along_x[pow_x] if pow_x else lead_z
            for pow_y in range(6 - pow_z - pow_x):
                term = lead * along_y[pow_y] if pow_y else lead
                part = (term[:, 0:128] + term[:, 128:256]) + (term[:, 256:384] + term[:, 384:512])
                moments[8 * channel : 8 * channel + 8, :] = part + pltpu.roll(part, 64, 1)
                channel += 1
    high, low = split(moments[...])
    lines = mxu(jnp.concatenate([high, low], axis=1), table[...])
    chunks[...] = jnp.zeros_like(chunks)
    for channel in range(MOMENTS):
        rows = lines[8 * channel : 8 * channel + 8]
        for block in range(8):
            chunks[block, :, channel * GROUP : (channel + 1) * GROUP] = rows[
                :, block * GROUP : (block + 1) * GROUP
            ]


def line_transform(lines, table, direction):
    high, low = split(lines)
    both = mxu(table, jnp.concatenate([high, high, low], axis=0))
    cos_part, sin_part = both[:N], both[N:]
    lane = lax.broadcasted_iota(jnp.int32, (1, LANES), 1)
    imag_lane = lax.rem(lane, GROUP) >= KEEP
    swapped = jnp.where(
        imag_lane, pltpu.roll(sin_part, KEEP, 1), pltpu.roll(sin_part, LANES - KEEP, 1)
    )
    factor = jnp.where(imag_lane, -1.0, 1.0) * direction
    return cos_part + swapped * factor


def y_forward_kernel(lines, table, out):
    result = line_transform(lines[...], table[...], 1.0)
    for piece in range(3):
        out[pl.ds(piece, N, stride=3), :] = result[:, 128 * piece : 128 * piece + 128]


def y_inverse_kernel(lines, table, out):
    gathered = jnp.concatenate([lines[pl.ds(piece, N, stride=3), :] for piece in range(3)], axis=1)
    out[...] = line_transform(gathered, table[...], -1.0)


def spectrum_kernel(lines, gains, forward, inverse, out, rows, spec, coeff):
    gathered = jnp.concatenate([lines[pl.ds(piece, N, stride=3), :] for piece in range(3)], axis=1)
    turned = jnp.concatenate([gathered, gathered], axis=0).T
    high, low = split(turned)
    rows[...] = mxu(jnp.concatenate([high, low], axis=1), forward[...])
    first_half = lax.broadcasted_iota(jnp.int32, (1, 128), 1) < N
    real_first, imag_first = [], []
    for kz in range(KEEP):
        real_part = rows[pl.ds(kz, MOMENTS, stride=GROUP), :]
        imag_part = rows[pl.ds(KEEP + kz, MOMENTS, stride=GROUP), :]
        both = jnp.where(first_half, real_part, -real_part) + pltpu.roll(imag_part, N, 1)
        real_first.append(both)
        imag_first.append(pltpu.roll(both, N, 1))
    real_first.append(real_first[-1])
    imag_first.append(imag_first[-1])
    for pair in range(3):
        where = slice(128 * pair, 128 * pair + 128)
        spec[0, :, where] = jnp.where(first_half, real_first[2 * pair], imag_first[2 * pair + 1])
        spec[1, :, where] = jnp.where(first_half, imag_first[2 * pair], real_first[2 * pair + 1])

    def add_channel(channel, running):
        real_sum, imag_sum = running
        gain_real = gains[channel, 0].astype(jnp.float32)
        gain_imag = gains[channel, 1].astype(jnp.float32)
        spec_real = spec[0, pl.ds(channel, 1), :]
        spec_imag = spec[1, pl.ds(channel, 1), :]
        real_sum = real_sum + (gain_real * spec_real - gain_imag * spec_imag)
        imag_sum = imag_sum + (gain_real * spec_imag + gain_imag * spec_real)
        return real_sum, imag_sum

    zero = jnp.zeros((MOMENTS, 128 * 3), jnp.float32)
    real_sum, imag_sum = lax.fori_loop(0, MOMENTS, add_channel, (zero, zero))
    coeff[...] = jnp.zeros_like(coeff)
    for pair in range(3):
        where = slice(128 * pair, 128 * pair + 128)
        real_part, imag_part = real_sum[:, where], imag_sum[:, where]
        real_roll, imag_roll = pltpu.roll(real_part, N, 1), pltpu.roll(imag_part, N, 1)
        for half in range(2):
            kz = 2 * pair + half
            if kz >= KEEP:
                continue
            low_real, high_real = (real_part, real_roll) if half == 0 else (real_roll, real_part)
            low_imag, high_imag = (imag_part, imag_roll) if half == 0 else (imag_roll, imag_part)
            coeff[pl.ds(kz, MOMENTS, stride=GROUP), :] = jnp.where(first_half, low_real, -high_imag)
            coeff[pl.ds(KEEP + kz, MOMENTS, stride=GROUP), :] = jnp.where(
                first_half, low_imag, high_real
            )
    high, low = split(coeff[...])
    result = mxu_nt(inverse[...], jnp.concatenate([high, high, low], axis=1))
    for piece in range(3):
        out[pl.ds(piece, N, stride=3), :] = result[:, 128 * piece : 128 * piece + 128]


def final_kernel(chunks, offsets, near, table, out, lines):
    lines[...] = jnp.zeros_like(lines)
    for channel in range(MOMENTS):
        for block in range(8):
            lines[8 * channel : 8 * channel + 8, block * GROUP : (block + 1) * GROUP] = chunks[
                block, :, channel * GROUP : (channel + 1) * GROUP
            ]
    high, low = split(lines[...])
    field = mxu(jnp.concatenate([high, low, high], axis=1), table[...])
    listed = channel_list()
    place = {powers_of: index for index, powers_of in enumerate(listed)}

    def coefficient(pow_x, pow_y, pow_z):
        index = place[(pow_x, pow_y, pow_z)]
        return field[8 * index : 8 * index + 8, :]

    for tile in range(4):
        where = slice(128 * tile, 128 * tile + 128)
        s = 2.0 * offsets[0, 0, :, where] - 1.0
        t = 2.0 * offsets[1, 0, :, where] - 1.0
        w = 2.0 * offsets[2, 0, :, where] - 1.0
        value, slope_s, slope_t = [], [], []
        for pow_z in range(2):
            inner, inner_slope = [], []
            for pow_x in range(6 - pow_z):
                top = 5 - pow_z - pow_x
                total = coefficient(pow_x, top, pow_z)
                slope = None
                for pow_y in range(top - 1, -1, -1):
                    slope = total if slope is None else slope * t + total
                    total = total * t + coefficient(pow_x, pow_y, pow_z)
                inner.append(total)
                inner_slope.append(slope)
            total, slope = inner[-1], None
            total_t = None
            for pow_x in range(len(inner) - 2, -1, -1):
                slope = total if slope is None else slope * s + total
                total = total * s + inner[pow_x]
                total_t = (
                    inner_slope[pow_x] if total_t is None else total_t * s + inner_slope[pow_x]
                )
            value.append(total)
            slope_s.append(slope)
            slope_t.append(total_t)
        out[0, 0, :, where] = near[0, :, where] - (slope_s[0] + w * slope_s[1])
        out[1, 0, :, where] = near[1, :, where] - (slope_t[0] + w * slope_t[1])
        out[2, 0, :, where] = near[2, :, where] - value[1]


def edge_kernel(before, own, after, first_rows, last_rows):
    for plane, ref in enumerate((before, own, after)):
        for comp in range(4):
            first_rows[4 * plane + comp : 4 * plane + comp + 1, :] = ref[comp, 0:1, :]
            last_rows[4 * plane + comp : 4 * plane + comp + 1, :] = ref[comp, 7:8, :]


def near_kernel(before, own, after, above, below, out, extended):
    for plane, ref in enumerate((before, own, after)):
        for comp in range(4):
            index = 4 * plane + comp
            extended[plane, comp, 8:16, :] = ref[comp] + (float(plane - 1) if comp == 0 else 0.0)
            shift = float(plane - 1) if comp == 0 else 0.0
            extended[plane, comp, 7:8, :] = above[index : index + 1, :] + shift
            extended[plane, comp, 16:17, :] = below[index : index + 1, :] + shift
    first_half = lax.broadcasted_iota(jnp.int32, (8, 128), 1) < N
    lane_z = lax.rem(lax.broadcasted_iota(jnp.int32, (8, 128), 1), N)
    targets = [[own[comp, :, 128 * k : 128 * k + 128] for k in range(4)] for comp in range(3)]

    def add_plane(plane, sums):
        sums = list(sums)
        for shift_y in (-1, 0, 1):
            for pair in range(4):
                window = [
                    extended[plane, comp, 8 + shift_y : 16 + shift_y, 128 * pair : 128 * pair + 128]
                    for comp in range(4)
                ]
                window[1] = window[1] + float(shift_y)
                turned = [pltpu.roll(value, N, 1) for value in window]
                for half in range(2):
                    source = [
                        jnp.where(first_half, a, b) if half == 0 else jnp.where(first_half, b, a)
                        for a, b in zip(window, turned)
                    ]
                    for shift_z in (-1, 0, 1):
                        moved = source
                        if shift_z:
                            moved = [pltpu.roll(v, (128 - shift_z) % 128, 1) for v in source]
                            moved[2] = moved[2] + float(shift_z)
                        for k in range(4):
                            sep = [moved[comp] - targets[comp][k] for comp in range(3)]
                            squared = (sep[0] * sep[0] + sep[1] * sep[1]) + (
                                sep[2] * sep[2] + SOFTEN * SOFTEN
                            )
                            inverse = lax.rsqrt(squared)
                            weight = (moved[3] * inverse) * (inverse * inverse)
                            for comp in range(3):
                                sums[3 * k + comp] = sums[3 * k + comp] + sep[comp] * weight
        return tuple(sums)

    zero = jnp.zeros((8, 128), jnp.float32)
    sums = lax.fori_loop(0, 3, add_plane, (zero,) * 12)
    for k in range(4):
        for comp in range(3):
            out[comp, :, 128 * k : 128 * k + 128] = sums[3 * k + comp]


def shape(*dims, dtype=jnp.float32):
    return jax.ShapeDtypeStruct(dims, dtype)


def call(kernel, outs, scratch, cycles):
    block = pl.BlockSpec(memory_space=pltpu.VMEM)
    return pl.pallas_call(
        kernel,
        out_shape=outs,
        in_specs=[block] * (kernel.__code__.co_argcount - len(jax.tree.leaves(outs)) - len(scratch)),
        out_specs=jax.tree.map(lambda _: block, outs),
        scratch_shapes=scratch,
        compiler_params=pltpu.CompilerParams(vmem_limit_bytes=16 << 20),
        cost_estimate=pl.CostEstimate(flops=cycles * 1000, bytes_accessed=cycles, transcendentals=0),
    )


def shift_axis(value, axis, step):
    count = lax.axis_size(axis)
    return lax.ppermute(value, axis, [(i, (i + step) % count) for i in range(count)])


def exchange_rows(value, axis):
    rows = value.reshape(64, 1, LANES)
    rows = lax.all_to_all(rows, axis, split_axis=0, concat_axis=0, tiled=True)
    return rows.reshape(192, 128)


def stages(offsets, masses, kernel):
    gains = jnp.transpose(kernel[:, :, :, 0, :LANES], (2, 1, 0, 3))
    left = jnp.asarray(table_left())
    chunks, packed = call(
        moments_kernel,
        (shape(8, 8, LANES), shape(4, 8, 512)),
        [VMEM((8 * MOMENTS, 128), jnp.float32)],
        2000,
    )(offsets, masses, jnp.asarray(table_z_forward()))
    chunks = lax.all_to_all(chunks, "gy", split_axis=0, concat_axis=0, tiled=True)
    before = shift_axis(packed, "gx", 1)
    after = shift_axis(packed, "gx", -1)
    lines = call(y_forward_kernel, shape(192, 128), [], 1000)(chunks.reshape(N, LANES), left)
    lines = exchange_rows(lines, "gx")
    first_rows, last_rows = call(
        edge_kernel, (shape(12, 512), shape(12, 512)), [], 200
    )(before, packed, after)
    above = shift_axis(last_rows, "gy", 1)
    below = shift_axis(first_rows, "gy", -1)
    lines = call(
        spectrum_kernel,
        shape(192, 128),
        [
            VMEM((LANES, 128), jnp.float32),
            VMEM((2, MOMENTS, LANES), jnp.float32),
            VMEM((LANES, 128), jnp.float32),
        ],
        3000,
    )(lines, gains, jnp.asarray(table_x_forward()), jnp.asarray(table_x_inverse()))
    lines = exchange_rows(lines, "gx")
    near = call(
        near_kernel, shape(3, 8, 512), [VMEM((3, 4, 24, 512), jnp.float32)], 6000
    )(before, packed, after, above, below)
    lines = call(y_inverse_kernel, shape(N, LANES), [], 1000)(lines, left)
    chunks = lax.all_to_all(
        lines.reshape(8, 8, LANES), "gy", split_axis=0, concat_axis=0, tiled=True
    )
    return call(
        final_kernel, shape(3, 1, 8, 512), [VMEM((8 * MOMENTS, 128), jnp.float32)], 2000
    )(chunks, offsets, near, jnp.asarray(table_z_inverse()))


def solution(mesh):
    placed = (P(None, "gx", "gy", None), P("gx", "gy", None), P(None, None, None, "gx", "gy"))
    return jax.shard_map(
        stages, mesh=mesh, in_specs=placed, out_specs=P(None, "gx", "gy", None), check_vma=False
    )
```

time: 199 us -> 105 us (0.53)
  other arithmetic: 58.1 us -> 0 us
  local copies, waits for them, and re-layouts: 45.8 us -> 6.48 us
  blocking collectives: 0 us -> 32.5 us
  starting transfers between devices: 57.7 us -> 31.7 us
  matrix products: 9.58 us -> 0 us
  Pallas kernels: 0 us -> 9.08 us
    all_to_all x0 -> x2, blocking collectives: none -> 32.5 us  [the longest x1 17.9 us: exchange_rows(): rows = lax.all_to_all(rows, axis, split_axis=0, concat_axis=0, tiled=True)]
    mul x45 -> x0, other arithmetic: 25.4 us -> none  [the longest x43 25.3 us: near_field(): neighbour[3] * inverse_r * inverse_r * inverse_r]
    slice x37 -> x1, local copies, waits for them, and re-layouts: 17.9 us -> 2.92 us  [stages(): gains = jnp.transpose(kernel[:, :, :, 0, :LANES], (2, 1, 0, 3))]
    ppermute x4, starting transfers between devices: 26.6 us -> 12.1 us  [shift_axis(): lax.ppermute(value, axis, [(i, (i + step) % count) for i in range(count)])]
    all_to_all x4 -> x2, waiting for transfers between devices: 24.7 us -> 10.3 us  [the longest x1 10.3 us: exchange_rows(): rows = lax.all_to_all(rows, axis, split_axis=0, concat_axis=0, tiled=True)]
    ppermute x4, waiting for transfers between devices: 0.01 us -> 14.4 us  [shift_axis(): lax.ppermute(value, axis, [(i, (i + step) % count) for i in range(count)])]
    all_to_all x4 -> x2, starting transfers between devices: 31.1 us -> 19.6 us  [the longest x1 13.4 us: exchange_rows(): rows = lax.all_to_all(rows, axis, split_axis=0, concat_axis=0, tiled=True)]
    unnamed x182 -> x19, local copies, waits for them, and re-layouts: 14.2 us -> 3.56 us
  transfers between devices with their start and end apart: 8 -> 6, of which waited for: 2 -> 4; matrix products, arithmetic and copies ran while one was open for 38% -> 3% of each run, Pallas kernels for 0% -> 3%
where the time goes in v1:
time: 105 us
  blocking collectives  32.5 us (31%)
  starting transfers between devices  31.7 us (30%)
  waiting for transfers between devices  24.6 us (23%)
  Pallas kernels  9.08 us (9%)
  local copies, waits for them, and re-layouts  6.48 us (6%)
    all_to_all x1, blocking collectives, exchange_rows(): rows = lax.all_to_all(rows, axis, split_axis=0, concat_axis=0, tiled=True)  17.9 us
    all_to_all x1, blocking collectives, stages(): lax.all_to_all(chunks, 'gy', split_axis=0, concat_axis=0, tiled=True)  14.6 us
    ppermute x4, waiting for transfers between devices, shift_axis(): lax.ppermute(value, axis, [(i, (i + step) % count) for i in range(count)])  14.4 us
    all_to_all x1, starting transfers between devices, exchange_rows(): rows = lax.all_to_all(rows, axis, split_axis=0, concat_axis=0, tiled=True)  13.4 us
    ppermute x4, starting transfers between devices, shift_axis(): lax.ppermute(value, axis, [(i, (i + step) % count) for i in range(count)])  12.1 us
    all_to_all x1, waiting for transfers between devices, exchange_rows(): rows = lax.all_to_all(rows, axis, split_axis=0, concat_axis=0, tiled=True)  10.3 us
    all_to_all x1, starting transfers between devices, stages(): lax.all_to_all(lines.reshape(8, 8, LANES), 'gy', split_axis=0, concat_axi...  6.19 us
    unnamed x19, local copies, waits for them, and re-layouts  3.56 us
  transfers between devices with their start and end apart: 6, of which 4 were waited for; matrix products, arithmetic and copies ran while one was open for 3% of the time, Pallas kernels for 3%

profile of v1, /device:TPU:1, one launch (start us, length us, event | category | flops | bytes accessed | tf_op | source)
XLA Modules:
  0.0 104.6 jit_solution(4734540223605136162)
XLA Ops:
  0.0 0.8 copy-done.2
  0.8 0.8 copy-done.6
  1.6 0.7 copy-done.8
  2.4 0.6 shard_map.82
  2.9 14.6 %all_to_all.20 = f32[8,8,384]{2,1,0:T(8,128)S(1)} all-to-all(f32[8,8,384]{2,1,0:T(8,128)S(1)} %get-tuple-element.9), channel_id=1, replica_groups=mesh['gx'=64,'gy'=8] {'gy'}, dimensions={0} | all-to-all | bytes 196608 | tf_op jit(solution)/shard_map/all_to_all | solution.py:352
  17.5 0.8 copy-done
  18.3 0.9 shard_map.83
  19.3 13.4 %all-to-all-start.1 = ((f32[64,1,384]{2,1,0:T(1,128)}), f32[64,1,384]{2,1,0:T(1,128)S(1)}, u32[]{:S(2)}, u32[]{:S(2)}) async-start(f32[64,1,384]{2,1,0:T(1,128)} %bitcast.1), calls=%async_computation.1 | async-start | bytes 196608 | tf_op jit(solution)/shard_map/all_to_all | solution.py:339
  32.7 2.9 %slice.3 = bf16[36,2,36,1,384]{4,1,3,2,0:T(2,128)(2,1)S(1)} slice(bf16[36,2,36,1,512]{4,1,3,2,0:T(2,128)(2,1)} %param.10), slice={[0:36], [0:2], [0:36], [0:1], [0:384]} | slice | bytes 3981312 | tf_op jit(solution)/shard_map/slice | solution.py:344
  35.7 0.3 copy.15
  36.0 10.3 %all-to-all-done.1 = f32[64,1,384]{2,1,0:T(1,128)S(1)} async-done(((f32[64,1,384]{2,1,0:T(1,128)}), f32[64,1,384]{2,1,0:T(1,128)S(1)}, u32[]{:S(2)}, u32[]{:S(2)}) %all-to-all-start.1) | async-done | bytes 98336 | tf_op jit(solution)/shard_map/all_to_all | solution.py:339
  46.3 2.1 %shard_map.84 = f32[192,128]{1,0:T(8,128)S(1)} custom-call(f32[192,128]{1,0:T(8,128)S(1)} %bitcast.12, bf16[36,2,36,384]{3,2,1,0:T(8,128)(2,1)S(1)} %bitcast.11, bf16[256,128]{1,0:T(8,128)(2,1)S(1)} %copy-done.5, bf16[64,384]{1,0:T(8,128)(2,1)S(1)} %copy-done.7), custom_call_target="tpu_custom_call" | custom-call | flops 3000000 | bytes 3000 | tf_op jit(solution)/shard_map/pallas_call | solution.py:362
  48.3 17.9 %all_to_all.21 = f32[64,1,384]{2,1,0:T(1,128)S(1)} all-to-all(f32[64,1,384]{2,1,0:T(1,128)S(1)} %bitcast.13), channel_id=1, replica_groups=mesh['gx'=64,'gy'=8] {'gx'}, dimensions={0} | all-to-all | bytes 196608 | tf_op jit(solution)/shard_map/all_to_all | solution.py:339
  66.3 0.9 shard_map.85
  67.2 6.2 %all-to-all-start.3 = ((f32[8,8,384]{2,1,0:T(8,128)}), f32[8,8,384]{2,1,0:T(8,128)S(1)}, u32[]{:S(2)}, u32[]{:S(2)}) async-start(f32[8,8,384]{2,1,0:T(8,128)} %bitcast.7), calls=%async_computation.3 | async-start | bytes 196608 | tf_op jit(solution)/shard_map/all_to_all | solution.py:377
  73.4 3.2 %collective-permute-start.1 = (f32[4,8,512]{2,1,0:T(8,128)S(1)}, f32[4,8,512]{2,1,0:T(8,128)S(1)}, u32[]{:S(2)}, u32[]{:S(2)}) collective-permute-start(f32[4,8,512]{2,1,0:T(8,128)S(1)} %get-tuple-element.10.own), channel_id=1, source_target_pairs={{0,504},{8,0},{16,8},{24,16},{32,24},{40,32},{48,40},{56,48},{64,5... | collective-permute-start | bytes 196616 | tf_op jit(solution)/shard_map/ppermute | solution.py:334
  76.6 2.1 %collective-permute-start = (f32[4,8,512]{2,1,0:T(8,128)S(1)}, f32[4,8,512]{2,1,0:T(8,128)S(1)}, u32[]{:S(2)}, u32[]{:S(2)}) collective-permute-start(f32[4,8,512]{2,1,0:T(8,128)S(1)} %get-tuple-element.10.own), channel_id=1, source_target_pairs={{0,8},{8,16},{16,24},{24,32},{32,40},{40,48},{48,56},{56,64},{64,7... | collective-permute-start | bytes 196616 | tf_op jit(solution)/shard_map/ppermute | solution.py:334
  78.7 0.1 collective-permute-done.1.after
  78.8 11.0 %collective-permute-done.before = f32[4,8,512]{2,1,0:T(8,128)S(1)} collective-permute-done((f32[4,8,512]{2,1,0:T(8,128)S(1)}, f32[4,8,512]{2,1,0:T(8,128)S(1)}, u32[]{:S(2)}, u32[]{:S(2)}) %collective-permute-start) | collective-permute-done | bytes 65568 | tf_op jit(solution)/shard_map/ppermute | solution.py:334
  89.8 4.9 %collective-permute-start.2 = (f32[12,512]{1,0:T(8,128)S(1)}, f32[12,512]{1,0:T(8,128)S(1)}, u32[]{:S(2)}, u32[]{:S(2)}) collective-permute-start(f32[12,512]{1,0:T(8,128)S(1)} %get-tuple-element.11), channel_id=1, source_target_pairs={{0,1},{1,2},{2,3},{3,4},{4,5},{5,6},{6,7},{7,0},{8,9},{9,10},{10,1... | collective-permute-start | bytes 73736 | tf_op jit(solution)/shard_map/ppermute | solution.py:334
  94.7 1.9 %collective-permute-start.3 = (f32[12,512]{1,0:T(8,128)S(1)}, f32[12,512]{1,0:T(8,128)S(1)}, u32[]{:S(2)}, u32[]{:S(2)}) collective-permute-start(f32[12,512]{1,0:T(8,128)S(1)} %get-tuple-element.12), channel_id=1, source_target_pairs={{0,7},{1,0},{2,1},{3,2},{4,3},{5,4},{6,5},{7,6},{8,15},{9,8},{10,9... | collective-permute-start | bytes 73736 | tf_op jit(solution)/shard_map/ppermute | solution.py:334
  96.7 3.3 %collective-permute-done.3.below = f32[12,512]{1,0:T(8,128)S(1)} collective-permute-done((f32[12,512]{1,0:T(8,128)S(1)}, f32[12,512]{1,0:T(8,128)S(1)}, u32[]{:S(2)}, u32[]{:S(2)}) %collective-permute-start.3) | collective-permute-done | bytes 24608 | tf_op jit(solution)/shard_map/ppermute | solution.py:334
  100.0 3.4 %shard_map.87.near = f32[3,8,512]{2,1,0:T(8,128)S(1)} custom-call(f32[4,8,512]{2,1,0:T(8,128)S(1)} %collective-permute-done.before, f32[4,8,512]{2,1,0:T(8,128)S(1)} %get-tuple-element.10.own, f32[4,8,512]{2,1,0:T(8,128)S(1)} %collective-permute-done.1.after, f32[12,512]{1,0:T(8,128)S(1)} %collective-permute-done.2.above, ...), custom_call_target="tpu_custom_call" | custom-call | flops 6000000 | bytes 6000 | tf_op jit(solution)/shard_map/pallas_call | solution.py:373
  103.4 1.2 %shard_map.88 = f32[3,1,8,512]{3,2,1,0:T(8,128)} custom-call(f32[8,8,384]{2,1,0:T(8,128)S(1)} %all-to-all-done.3.chunks, f32[3,1,8,512]{3,2,1,0:T(8,128)S(1)} %copy-done.3, f32[3,8,512]{2,1,0:T(8,128)S(1)} %shard_map.87.near, bf16[384,128]{1,0:T(8,128)(2,1)S(1)} %copy-done.4), custom_call_target="tpu_custom_call" | custom-call | flops 2000000 | bytes 2000 | tf_op jit(solution)/shard_map/pallas_call | solution.py:380
  (17 shorter events, 0.1 us)
Async XLA Ops:
  0.0 0.8 copy-start.2
  0.8 0.8 copy-start.6
  1.6 0.7 copy-start.8
  17.5 0.8 copy-start
  19.3 27.0 %all-to-all-start.1 = ((f32[64,1,384]{2,1,0:T(1,128)}), f32[64,1,384]{2,1,0:T(1,128)S(1)}, u32[]{:S(2)}, u32[]{:S(2)}) async-start(f32[64,1,384]{2,1,0:T(1,128)} %bitcast.1), calls=%async_computation.1 | async-start | bytes 196608 | tf_op jit(solution)/shard_map/all_to_all | solution.py:339
  35.6 10.7 %copy-start.5 = (bf16[256,128]{1,0:T(8,128)(2,1)S(1)}, bf16[256,128]{1,0:T(8,128)(2,1)}, u32[]{:S(2)}) copy-start(bf16[256,128]{1,0:T(8,128)(2,1)} %constant.12.clone.forward) | copy-start | bytes 196612
  35.6 10.6 %copy-start.7 = (bf16[64,384]{1,0:T(8,128)(2,1)S(1)}, bf16[64,384]{1,0:T(8,128)(2,1)}, u32[]{:S(2)}) copy-start(bf16[64,384]{1,0:T(8,128)(2,1)} %constant.13.clone.inverse) | copy-start | bytes 147460
  36.0 30.3 %copy-start.1 = (bf16[128,192]{1,0:T(8,128)(2,1)S(1)}, bf16[128,192]{1,0:T(8,128)(2,1)}, u32[]{:S(2)}) copy-start(bf16[128,192]{1,0:T(8,128)(2,1)} %constant.10.clone.table) | copy-start | bytes 147460
  36.0 67.4 %copy-start.3 = (f32[3,1,8,512]{3,2,1,0:T(8,128)S(1)}, f32[3,1,8,512]{3,2,1,0:T(8,128)}, u32[]{:S(2)}) copy-start(f32[3,1,8,512]{3,2,1,0:T(8,128)} %offsets.3) | copy-start | bytes 147460
  36.0 67.4 %copy-start.4 = (bf16[384,128]{1,0:T(8,128)(2,1)S(1)}, bf16[384,128]{1,0:T(8,128)(2,1)}, u32[]{:S(2)}) copy-start(bf16[384,128]{1,0:T(8,128)(2,1)} %constant.14.clone.table) | copy-start | bytes 294916
  67.2 36.1 %all-to-all-start.3 = ((f32[8,8,384]{2,1,0:T(8,128)}), f32[8,8,384]{2,1,0:T(8,128)S(1)}, u32[]{:S(2)}, u32[]{:S(2)}) async-start(f32[8,8,384]{2,1,0:T(8,128)} %bitcast.7), calls=%async_computation.3 | async-start | bytes 196608 | tf_op jit(solution)/shard_map/all_to_all | solution.py:377
  73.4 5.4 %collective-permute-start.1 = (f32[4,8,512]{2,1,0:T(8,128)S(1)}, f32[4,8,512]{2,1,0:T(8,128)S(1)}, u32[]{:S(2)}, u32[]{:S(2)}) collective-permute-start(f32[4,8,512]{2,1,0:T(8,128)S(1)} %get-tuple-element.10.own), channel_id=1, source_target_pairs={{0,504},{8,0},{16,8},{24,16},{32,24},{40,32},{48,40},{56,48},{64,5... | collective-permute-start | bytes 196616 | tf_op jit(solution)/shard_map/ppermute | solution.py:334
  76.6 13.2 %collective-permute-start = (f32[4,8,512]{2,1,0:T(8,128)S(1)}, f32[4,8,512]{2,1,0:T(8,128)S(1)}, u32[]{:S(2)}, u32[]{:S(2)}) collective-permute-start(f32[4,8,512]{2,1,0:T(8,128)S(1)} %get-tuple-element.10.own), channel_id=1, source_target_pairs={{0,8},{8,16},{16,24},{24,32},{32,40},{40,48},{48,56},{56,64},{64,7... | collective-permute-start | bytes 196616 | tf_op jit(solution)/shard_map/ppermute | solution.py:334
  89.8 6.9 %collective-permute-start.2 = (f32[12,512]{1,0:T(8,128)S(1)}, f32[12,512]{1,0:T(8,128)S(1)}, u32[]{:S(2)}, u32[]{:S(2)}) collective-permute-start(f32[12,512]{1,0:T(8,128)S(1)} %get-tuple-element.11), channel_id=1, source_target_pairs={{0,1},{1,2},{2,3},{3,4},{4,5},{5,6},{6,7},{7,0},{8,9},{9,10},{10,1... | collective-permute-start | bytes 73736 | tf_op jit(solution)/shard_map/ppermute | solution.py:334
  94.7 5.2 %collective-permute-start.3 = (f32[12,512]{1,0:T(8,128)S(1)}, f32[12,512]{1,0:T(8,128)S(1)}, u32[]{:S(2)}, u32[]{:S(2)}) collective-permute-start(f32[12,512]{1,0:T(8,128)S(1)} %get-tuple-element.12), channel_id=1, source_target_pairs={{0,7},{1,0},{2,1},{3,2},{4,3},{5,4},{6,5},{7,6},{8,15},{9,8},{10,9... | collective-permute-start | bytes 73736 | tf_op jit(solution)/shard_map/ppermute | solution.py:334

commit v2 on v1

--- a/solution.py
+++ b/solution.py
@@ -100,11 +100,53 @@
     return result
 
 
-def moments_kernel(offsets, masses, table, chunks, packed, moments):
+EDGE = 256
+ROWS = 4 * 10
+
+
+def edge_places(comp):
+    for tile in range(4):
+        index = 4 * comp + tile
+        lane = LANES + 128 * (index % 2)
+        yield tile, index // 2, slice(lane, lane + 128)
+
+
+def moments_kernel(
+    offsets_hbm,
+    masses_hbm,
+    table_hbm,
+    left_hbm,
+    chunks,
+    packed,
+    left,
+    offsets,
+    masses,
+    table,
+    moments,
+    sems,
+):
+    pairs = (
+        (offsets_hbm, offsets),
+        (masses_hbm, masses),
+        (table_hbm, table),
+        (left_hbm, left),
+    )
+    copies = [pltpu.make_async_copy(a, b, sems.at[i]) for i, (a, b) in enumerate(pairs)]
+    for copy in copies:
+        copy.start()
+    me = lax.axis_index("gy")
+    after, before = lax.rem(me + 1, 8), lax.rem(me + 7, 8)
+    chunks[:, :, 256:] = jnp.zeros((8, 8, LANES + EDGE - 256), jnp.float32)
+    copies[0].wait()
+    copies[1].wait()
     mass = masses[0]
-    for comp in range(3):
-        packed[comp] = offsets[comp, 0]
-    packed[3] = mass
+    for comp in range(4):
+        value = offsets[comp, 0] if comp < 3 else mass
+        for tile, row, lanes in edge_places(comp):
+            part = value[:, 128 * tile : 128 * tile + 128]
+            packed[tile, pl.ds(comp, 8, stride=4), :] = part
+            chunks[after, row : row + 1, lanes] = part[7:8]
+            chunks[before, row : row + 1, lanes] = part[0:1]
     along_x = powers(2.0 * offsets[0, 0] - 1.0, 5)
     along_y = powers(2.0 * offsets[1, 0] - 1.0, 5)
     along_z = 2.0 * offsets[2, 0] - 1.0
@@ -119,14 +161,15 @@
                 moments[8 * channel : 8 * channel + 8, :] = part + pltpu.roll(part, 64, 1)
                 channel += 1
     high, low = split(moments[...])
+    copies[2].wait()
     lines = mxu(jnp.concatenate([high, low], axis=1), table[...])
-    chunks[...] = jnp.zeros_like(chunks)
     for channel in range(MOMENTS):
         rows = lines[8 * channel : 8 * channel + 8]
         for block in range(8):
             chunks[block, :, channel * GROUP : (channel + 1) * GROUP] = rows[
                 :, block * GROUP : (block + 1) * GROUP
             ]
+    copies[3].wait()
 
 
 def line_transform(lines, table, direction):
@@ -142,10 +185,18 @@
     return cos_part + swapped * factor
 
 
-def y_forward_kernel(lines, table, out):
-    result = line_transform(lines[...], table[...], 1.0)
+def y_forward_kernel(chunks, packed, table, out, extended):
+    result = line_transform(chunks[:, :, :LANES].reshape(N, LANES), table[...], 1.0)
     for piece in range(3):
         out[pl.ds(piece, N, stride=3), :] = result[:, 128 * piece : 128 * piece + 128]
+    me = lax.axis_index("gy")
+    after, before = lax.rem(me + 1, 8), lax.rem(me + 7, 8)
+    extended[:, 4 : ROWS - 4, :] = packed[...]
+    for comp in range(4):
+        last = ROWS - 4 + comp
+        for tile, row, lanes in edge_places(comp):
+            extended[tile, comp : comp + 1, :] = chunks[before, row : row + 1, lanes]
+            extended[tile, last : last + 1, :] = chunks[after, row : row + 1, lanes]
 
 
 def y_inverse_kernel(lines, table, out):
@@ -255,33 +306,24 @@
         out[2, 0, :, where] = near[2, :, where] - value[1]
 
 
-def edge_kernel(before, own, after, first_rows, last_rows):
+def near_kernel(before, own, after, out, planes):
     for plane, ref in enumerate((before, own, after)):
-        for comp in range(4):
-            first_rows[4 * plane + comp : 4 * plane + comp + 1, :] = ref[comp, 0:1, :]
-            last_rows[4 * plane + comp : 4 * plane + comp + 1, :] = ref[comp, 7:8, :]
-
-
-def near_kernel(before, own, after, above, below, out, extended):
-    for plane, ref in enumerate((before, own, after)):
-        for comp in range(4):
-            index = 4 * plane + comp
-            extended[plane, comp, 8:16, :] = ref[comp] + (float(plane - 1) if comp == 0 else 0.0)
-            shift = float(plane - 1) if comp == 0 else 0.0
-            extended[plane, comp, 7:8, :] = above[index : index + 1, :] + shift
-            extended[plane, comp, 16:17, :] = below[index : index + 1, :] + shift
+        planes[plane] = ref[...]
     first_half = lax.broadcasted_iota(jnp.int32, (8, 128), 1) < N
-    lane_z = lax.rem(lax.broadcasted_iota(jnp.int32, (8, 128), 1), N)
-    targets = [[own[comp, :, 128 * k : 128 * k + 128] for k in range(4)] for comp in range(3)]
+    targets = [
+        [own[k, pl.ds(4 + comp, 8, stride=4), :] for k in range(4)]
+        for comp in range(3)
+    ]
 
     def add_plane(plane, sums):
         sums = list(sums)
         for shift_y in (-1, 0, 1):
             for pair in range(4):
                 window = [
-                    extended[plane, comp, 8 + shift_y : 16 + shift_y, 128 * pair : 128 * pair + 128]
+                    planes[plane, pair, pl.ds(4 + 4 * shift_y + comp, 8, stride=4), :]
                     for comp in range(4)
                 ]
+                window[0] = window[0] + (plane - 1).astype(jnp.float32)
                 window[1] = window[1] + float(shift_y)
                 turned = [pltpu.roll(value, N, 1) for value in window]
                 for half in range(2):
@@ -316,17 +358,23 @@
     return jax.ShapeDtypeStruct(dims, dtype)
 
 
-def call(kernel, outs, scratch, cycles):
+def call(kernel, outs, scratch, cycles, in_specs=None, out_specs=None, aliases={}):
     block = pl.BlockSpec(memory_space=pltpu.VMEM)
+    count = kernel.__code__.co_argcount - len(jax.tree.leaves(outs)) - len(scratch)
     return pl.pallas_call(
         kernel,
         out_shape=outs,
-        in_specs=[block] * (kernel.__code__.co_argcount - len(jax.tree.leaves(outs)) - len(scratch)),
-        out_specs=jax.tree.map(lambda _: block, outs),
+        in_specs=in_specs or [block] * count,
+        out_specs=out_specs or jax.tree.map(lambda _: block, outs),
+        input_output_aliases=aliases,
         scratch_shapes=scratch,
         compiler_params=pltpu.CompilerParams(vmem_limit_bytes=16 << 20),
         cost_estimate=pl.CostEstimate(flops=cycles * 1000, bytes_accessed=cycles, transcendentals=0),
     )
+
+
+def far_memory(value):
+    return pltpu.with_memory_space_constraint(jnp.asarray(value), pltpu.HBM)
 
 
 def shift_axis(value, axis, step):
@@ -341,24 +389,36 @@
 
 
 def stages(offsets, masses, kernel):
-    gains = jnp.transpose(kernel[:, :, :, 0, :LANES], (2, 1, 0, 3))
-    left = jnp.asarray(table_left())
-    chunks, packed = call(
+    hbm = pl.BlockSpec(memory_space=pltpu.HBM)
+    table_z, table_y = table_z_forward(), table_left()
+    gains = kernel[:, :, :, 0, :LANES]
+    chunks, packed, left = call(
         moments_kernel,
-        (shape(8, 8, LANES), shape(4, 8, 512)),
-        [VMEM((8 * MOMENTS, 128), jnp.float32)],
+        (
+            shape(8, 8, LANES + EDGE),
+            shape(4, 32, 128),
+            shape(*table_y.shape, dtype=jnp.bfloat16),
+        ),
+        [
+            VMEM((3, 1, 8, 512), jnp.float32),
+            VMEM((1, 8, 512), jnp.float32),
+            VMEM(table_z.shape, jnp.bfloat16),
+            VMEM((8 * MOMENTS, 128), jnp.float32),
+            pltpu.SemaphoreType.DMA((4,)),
+        ],
         2000,
-    )(offsets, masses, jnp.asarray(table_z_forward()))
+        [hbm] * 4,
+    )(*(far_memory(value) for value in (offsets, masses, table_z, table_y)))
+    chunks, gains = lax.optimization_barrier((chunks, gains))
+    gains = jnp.transpose(gains, (2, 1, 0, 3))
+    chunks, gains = lax.optimization_barrier((chunks, gains))
     chunks = lax.all_to_all(chunks, "gy", split_axis=0, concat_axis=0, tiled=True)
-    before = shift_axis(packed, "gx", 1)
-    after = shift_axis(packed, "gx", -1)
-    lines = call(y_forward_kernel, shape(192, 128), [], 1000)(chunks.reshape(N, LANES), left)
+    lines, extended = call(
+        y_forward_kernel, (shape(192, 128), shape(4, ROWS, 128)), [], 1000
+    )(chunks, packed, left)
     lines = exchange_rows(lines, "gx")
-    first_rows, last_rows = call(
-        edge_kernel, (shape(12, 512), shape(12, 512)), [], 200
-    )(before, packed, after)
-    above = shift_axis(last_rows, "gy", 1)
-    below = shift_axis(first_rows, "gy", -1)
+    before = shift_axis(extended, "gx", 1)
+    after = shift_axis(extended, "gx", -1)
     lines = call(
         spectrum_kernel,
         shape(192, 128),
@@ -370,9 +430,9 @@
         3000,
     )(lines, gains, jnp.asarray(table_x_forward()), jnp.asarray(table_x_inverse()))
     lines = exchange_rows(lines, "gx")
-    near = call(
-        near_kernel, shape(3, 8, 512), [VMEM((3, 4, 24, 512), jnp.float32)], 6000
-    )(before, packed, after, above, below)
+    near = call(near_kernel, shape(3, 8, 512), [VMEM((3, 4, ROWS, 128), jnp.float32)], 6000)(
+        before, extended, after
+    )
     lines = call(y_inverse_kernel, shape(N, LANES), [], 1000)(lines, left)
     chunks = lax.all_to_all(
         lines.reshape(8, 8, LANES), "gy", split_axis=0, concat_axis=0, tiled=True

time: 105 us -> 96.2 us (0.916); the launches traced: 105 us -> 94.3 us
  blocking collectives: 32.5 us -> 59.3 us
  starting transfers between devices: 31.7 us -> 12.2 us
  waiting for transfers between devices: 24.6 us -> 11.7 us
  local copies, waits for them, and re-layouts: 6.48 us -> 1.9 us
    all_to_all x1 -> x2, blocking collectives: 17.9 us -> 44 us  [exchange_rows(): rows = lax.all_to_all(rows, axis, split_axis=0, concat_axis=0, tiled=True)]
    all_to_all x1 -> x0, starting transfers between devices: 13.4 us -> none  [exchange_rows(): rows = lax.all_to_all(rows, axis, split_axis=0, concat_axis=0, tiled=True)]
    all_to_all x1 -> x0, waiting for transfers between devices: 10.3 us -> none  [exchange_rows(): rows = lax.all_to_all(rows, axis, split_axis=0, concat_axis=0, tiled=True)]
    ppermute x4 -> x2, starting transfers between devices: 12.1 us -> 5.28 us  [shift_axis(): lax.ppermute(value, axis, [(i, (i + step) % count) for i in range(count)])]
    unnamed x19 -> x9, local copies, waits for them, and re-layouts: 3.56 us -> 0.35 us
    ppermute x4 -> x2, waiting for transfers between devices: 14.4 us -> 11.7 us  [shift_axis(): lax.ppermute(value, axis, [(i, (i + step) % count) for i in range(count)])]
    slice x1 -> x2, local copies, waits for them, and re-layouts: 2.92 us -> 1.55 us  [stages(): gains = kernel[:, :, :, 0, :LANES]]
    pallas_call x4 -> x3, Pallas kernels: 4.89 us -> 4.92 us  [the longest x1 3.11 us: stages(): call(near_kernel, shape(3, 8, 512), [VMEM((3, 4, ROWS, 128), jnp.float32)...]
  transfers between devices with their start and end apart: 6 -> 3, of which waited for: 4 -> 2; matrix products, arithmetic and copies ran while one was open for 3% -> 0% of each run, Pallas kernels for 3% -> 3%
where the time goes in v2:
time: 96.2 us; the launch traced here: 94.3 us
  blocking collectives  59.3 us (62%)
  starting transfers between devices  12.2 us (13%)
  waiting for transfers between devices  11.7 us (12%)
  Pallas kernels  9.1 us (9%)
  local copies, waits for them, and re-layouts  1.9 us (2%)
    all_to_all x2, blocking collectives, exchange_rows(): rows = lax.all_to_all(rows, axis, split_axis=0, concat_axis=0, tiled=True)  44 us
    all_to_all x1, blocking collectives, stages(): lax.all_to_all(chunks, 'gy', split_axis=0, concat_axis=0, tiled=True)  15.3 us
    ppermute x2, waiting for transfers between devices, shift_axis(): lax.ppermute(value, axis, [(i, (i + step) % count) for i in range(count)])  11.7 us
    all_to_all x1, starting transfers between devices, stages(): lax.all_to_all(lines.reshape(8, 8, LANES), 'gy', split_axis=0, concat_axi...  6.96 us
    ppermute x2, starting transfers between devices, shift_axis(): lax.ppermute(value, axis, [(i, (i + step) % count) for i in range(count)])  5.28 us
    pallas_call x1, Pallas kernels, stages(): call(near_kernel, shape(3, 8, 512), [VMEM((3, 4, ROWS, 128), jnp.float32)...  3.11 us
    pallas_call x1, Pallas kernels, stages(): call(spectrum_kernel, shape(192, 128), [VMEM((LANES, 128), jnp.float32),...  2.06 us
  transfers between devices with their start and end apart: 3, of which 2 were waited for; matrix products, arithmetic and copies ran while one was open for 0% of the time, Pallas kernels for 3%

profile of v2, /device:TPU:1, one launch (start us, length us, event | category | flops | bytes accessed | tf_op | source)
XLA Modules:
  0.0 94.3 jit_solution(15080743613823292791)
XLA Ops:
  0.0 1.6 %slice-done = bf16[36,2,36,1,384]{4,1,3,2,0:T(2,128)(2,1)S(1)} async-done(((bf16[36,2,36,1,512]{4,1,3,2,0:T(2,128)(2,1)}), bf16[36,2,36,1,384]{4,1,3,2,0:T(2,128)(2,1)S(1)}, s32[]{:S(2)}) %slice-start) | async-done | bytes 1990680 | tf_op jit(solution)/shard_map/slice | solution.py:394
  1.6 0.0 copy-start.2
  1.6 0.3 copy.15
  1.9 0.0 copy-start
  1.9 0.0 copy-start.1
  1.9 1.5 %shard_map.82 = (f32[8,8,640]{2,1,0:T(8,128)S(1)}, f32[4,32,128]{2,1,0:T(8,128)S(1)}, bf16[128,192]{1,0:T(8,128)(2,1)S(1)}) custom-call(f32[3,1,8,512]{3,2,1,0:T(8,128)} %offsets.1, f32[1,8,512]{2,1,0:T(8,128)} %masses_hbm.1, bf16[256,128]{1,0:T(8,128)(2,1)} %constant.10.clone.table_hbm, bf16[128,192]{1,0:T(8,128)(2,1)} %constant.11.clone.left_hbm), custom_call_target="tpu_custom_call" | custom-call | flops 2000000 | bytes 2000 | tf_op jit(solution)/shard_map/pallas_call | solution.py:395
  3.5 15.3 %all_to_all.20.chunks = f32[8,8,640]{2,1,0:T(8,128)S(1)} all-to-all(f32[8,8,640]{2,1,0:T(8,128)S(1)} %get-tuple-element.17), channel_id=1, replica_groups=mesh['gx'=64,'gy'=8] {'gy'}, dimensions={0} | all-to-all | bytes 327680 | tf_op jit(solution)/shard_map/all_to_all | solution.py:415
  18.7 0.3 shard_map.83
  19.0 26.8 %all_to_all.21 = f32[64,1,384]{2,1,0:T(1,128)S(1)} all-to-all(f32[64,1,384]{2,1,0:T(1,128)S(1)} %bitcast.13), channel_id=1, replica_groups=mesh['gx'=64,'gy'=8] {'gx'}, dimensions={0} | all-to-all | bytes 196608 | tf_op jit(solution)/shard_map/all_to_all | solution.py:387
  45.8 0.0 copy-done.2
  45.8 0.0 copy-done.3
  45.8 2.1 %shard_map.84 = f32[192,128]{1,0:T(8,128)S(1)} custom-call(f32[192,128]{1,0:T(8,128)S(1)} %bitcast.10, bf16[36,2,36,384]{3,2,1,0:T(8,128)(2,1)S(1)} %bitcast.9, bf16[256,128]{1,0:T(8,128)(2,1)S(1)} %copy-done.2, bf16[64,384]{1,0:T(8,128)(2,1)S(1)} %copy-done.3), custom_call_target="tpu_custom_call" | custom-call | flops 3000000 | bytes 3000 | tf_op jit(solution)/shard_map/pallas_call | solution.py:422
  47.9 17.2 %all_to_all.22 = f32[64,1,384]{2,1,0:T(1,128)S(1)} all-to-all(f32[64,1,384]{2,1,0:T(1,128)S(1)} %bitcast.11), channel_id=1, replica_groups=mesh['gx'=64,'gy'=8] {'gx'}, dimensions={0} | all-to-all | bytes 196608 | tf_op jit(solution)/shard_map/all_to_all | solution.py:387
  65.1 0.9 shard_map.85
  66.1 7.0 %all-to-all-start.3 = ((f32[8,8,384]{2,1,0:T(8,128)}), f32[8,8,384]{2,1,0:T(8,128)S(1)}, u32[]{:S(2)}, u32[]{:S(2)}) async-start(f32[8,8,384]{2,1,0:T(8,128)} %bitcast.6), calls=%async_computation.3 | async-start | bytes 196608 | tf_op jit(solution)/shard_map/all_to_all | solution.py:437
  73.0 3.4 %collective-permute-start.1 = (f32[4,40,128]{2,1,0:T(8,128)S(1)}, f32[4,40,128]{2,1,0:T(8,128)S(1)}, u32[]{:S(2)}, u32[]{:S(2)}) collective-permute-start(f32[4,40,128]{2,1,0:T(8,128)S(1)} %get-tuple-element.22.own), channel_id=1, source_target_pairs={{0,504},{8,0},{16,8},{24,16},{32,24},{40,32},{48,40},{56,48},{64,5... | collective-permute-start | bytes 245768 | tf_op jit(solution)/shard_map/ppermute | solution.py:382
  76.4 1.9 %collective-permute-start = (f32[4,40,128]{2,1,0:T(8,128)S(1)}, f32[4,40,128]{2,1,0:T(8,128)S(1)}, u32[]{:S(2)}, u32[]{:S(2)}) collective-permute-start(f32[4,40,128]{2,1,0:T(8,128)S(1)} %get-tuple-element.22.own), channel_id=1, source_target_pairs={{0,8},{8,16},{16,24},{24,32},{32,40},{40,48},{48,56},{56,64},{64,7... | collective-permute-start | bytes 245768 | tf_op jit(solution)/shard_map/ppermute | solution.py:382
  78.3 0.5 collective-permute-done.1.after
  78.8 11.2 %collective-permute-done.before = f32[4,40,128]{2,1,0:T(8,128)S(1)} collective-permute-done((f32[4,40,128]{2,1,0:T(8,128)S(1)}, f32[4,40,128]{2,1,0:T(8,128)S(1)}, u32[]{:S(2)}, u32[]{:S(2)}) %collective-permute-start) | collective-permute-done | bytes 81952 | tf_op jit(solution)/shard_map/ppermute | solution.py:382
  90.0 3.1 %shard_map.86.near = f32[3,8,512]{2,1,0:T(8,128)S(1)} custom-call(f32[4,40,128]{2,1,0:T(8,128)S(1)} %collective-permute-done.before, f32[4,40,128]{2,1,0:T(8,128)S(1)} %get-tuple-element.22.own, f32[4,40,128]{2,1,0:T(8,128)S(1)} %collective-permute-done.1.after), custom_call_target="tpu_custom_call" | custom-call | flops 6000000 | bytes 6000 | tf_op jit(solution)/shard_map/pallas_call | solution.py:433
  93.1 0.0 all-to-all-done.3.chunks
  93.1 0.0 copy-done
  93.1 0.0 copy-done.1
  93.1 1.2 %shard_map.87 = f32[3,1,8,512]{3,2,1,0:T(8,128)} custom-call(f32[8,8,384]{2,1,0:T(8,128)S(1)} %all-to-all-done.3.chunks, f32[3,1,8,512]{3,2,1,0:T(8,128)S(1)} %copy-done, f32[3,8,512]{2,1,0:T(8,128)S(1)} %shard_map.86.near, bf16[384,128]{1,0:T(8,128)(2,1)S(1)} %copy-done.1), custom_call_target="tpu_custom_call" | custom-call | flops 2000000 | bytes 2000 | tf_op jit(solution)/shard_map/pallas_call | solution.py:440
  (2 shorter events, 0.0 us)
Async XLA Ops:
  0.0 1.6 %slice-start = ((bf16[36,2,36,1,512]{4,1,3,2,0:T(2,128)(2,1)}), bf16[36,2,36,1,384]{4,1,3,2,0:T(2,128)(2,1)S(1)}, s32[]{:S(2)}) async-start(bf16[36,2,36,1,512]{4,1,3,2,0:T(2,128)(2,1)} %param.10), calls=%async_computation.4 | async-start | bytes 3981312 | tf_op jit(solution)/shard_map/slice | solution.py:394
  1.6 44.3 %copy-start.2 = (bf16[256,128]{1,0:T(8,128)(2,1)S(1)}, bf16[256,128]{1,0:T(8,128)(2,1)}, u32[]{:S(2)}) copy-start(bf16[256,128]{1,0:T(8,128)(2,1)} %constant.12.clone.forward) | copy-start | bytes 196612
  1.6 44.3 %copy-start.3 = (bf16[64,384]{1,0:T(8,128)(2,1)S(1)}, bf16[64,384]{1,0:T(8,128)(2,1)}, u32[]{:S(2)}) copy-start(bf16[64,384]{1,0:T(8,128)(2,1)} %constant.13.clone.inverse) | copy-start | bytes 147460
  1.9 91.2 %copy-start = (f32[3,1,8,512]{3,2,1,0:T(8,128)S(1)}, f32[3,1,8,512]{3,2,1,0:T(8,128)}, u32[]{:S(2)}) copy-start(f32[3,1,8,512]{3,2,1,0:T(8,128)} %offsets.1) | copy-start | bytes 147460
  1.9 91.2 %copy-start.1 = (bf16[384,128]{1,0:T(8,128)(2,1)S(1)}, bf16[384,128]{1,0:T(8,128)(2,1)}, u32[]{:S(2)}) copy-start(bf16[384,128]{1,0:T(8,128)(2,1)} %constant.14.clone.table) | copy-start | bytes 294916
  66.1 27.1 %all-to-all-start.3 = ((f32[8,8,384]{2,1,0:T(8,128)}), f32[8,8,384]{2,1,0:T(8,128)S(1)}, u32[]{:S(2)}, u32[]{:S(2)}) async-start(f32[8,8,384]{2,1,0:T(8,128)} %bitcast.6), calls=%async_computation.3 | async-start | bytes 196608 | tf_op jit(solution)/shard_map/all_to_all | solution.py:437
  73.0 5.8 %collective-permute-start.1 = (f32[4,40,128]{2,1,0:T(8,128)S(1)}, f32[4,40,128]{2,1,0:T(8,128)S(1)}, u32[]{:S(2)}, u32[]{:S(2)}) collective-permute-start(f32[4,40,128]{2,1,0:T(8,128)S(1)} %get-tuple-element.22.own), channel_id=1, source_target_pairs={{0,504},{8,0},{16,8},{24,16},{32,24},{40,32},{48,40},{56,48},{64,5... | collective-permute-start | bytes 245768 | tf_op jit(solution)/shard_map/ppermute | solution.py:382
  76.4 13.6 %collective-permute-start = (f32[4,40,128]{2,1,0:T(8,128)S(1)}, f32[4,40,128]{2,1,0:T(8,128)S(1)}, u32[]{:S(2)}, u32[]{:S(2)}) collective-permute-start(f32[4,40,128]{2,1,0:T(8,128)S(1)} %get-tuple-element.22.own), channel_id=1, source_target_pairs={{0,8},{8,16},{16,24},{24,32},{32,40},{40,48},{48,56},{56,64},{64,7... | collective-permute-start | bytes 245768 | tf_op jit(solution)/shard_map/ppermute | solution.py:382

commit v3 on v2

--- a/solution.py
+++ b/solution.py
@@ -101,7 +101,12 @@
 
 
 EDGE = 256
-ROWS = 4 * 10
+LEAD = 3
+ROWS = 48
+FIRST_OWN = LEAD + 4
+LAST_EDGE = LEAD + 36
+PIECE = 5
+CHUNK = 8
 
 
 def edge_places(comp):
@@ -185,27 +190,57 @@
     return cos_part + swapped * factor
 
 
+def first_half_lanes():
+    return lax.broadcasted_iota(jnp.int32, (CHUNK, 128), 1) < N
+
+
+def pieces():
+    for tile in range(4):
+        for group in range(7, -1, -1):
+            first = 8 * tile + group
+            yield tile, PIECE * group, CHUNK * first, CHUNK * (first + 32)
+
+
+def gather_lines(lines):
+    return jnp.concatenate([lines[pl.ds(row, N, stride=CHUNK), :] for row in range(LEAD)], axis=1)
+
+
+def scatter_lines(out, result):
+    for row in range(LEAD):
+        out[pl.ds(row, N, stride=CHUNK), :] = result[:, 128 * row : 128 * row + 128]
+
+
 def y_forward_kernel(chunks, packed, table, out, extended):
-    result = line_transform(chunks[:, :, :LANES].reshape(N, LANES), table[...], 1.0)
-    for piece in range(3):
-        out[pl.ds(piece, N, stride=3), :] = result[:, 128 * piece : 128 * piece + 128]
     me = lax.axis_index("gy")
     after, before = lax.rem(me + 1, 8), lax.rem(me + 7, 8)
-    extended[:, 4 : ROWS - 4, :] = packed[...]
+    extended[:, FIRST_OWN:LAST_EDGE, :] = packed[...]
     for comp in range(4):
-        last = ROWS - 4 + comp
+        top, bottom = LEAD + comp, LAST_EDGE + comp
         for tile, row, lanes in edge_places(comp):
-            extended[tile, comp : comp + 1, :] = chunks[before, row : row + 1, lanes]
-            extended[tile, last : last + 1, :] = chunks[after, row : row + 1, lanes]
+            extended[tile, top : top + 1, :] = chunks[before, row : row + 1, lanes]
+            extended[tile, bottom : bottom + 1, :] = chunks[after, row : row + 1, lanes]
+    result = line_transform(chunks[:, :, :LANES].reshape(N, LANES), table[...], 1.0)
+    half = first_half_lanes()
+    for tile, start, low, high in pieces():
+        value = extended[tile, start : start + CHUNK, :]
+        turned = pltpu.roll(value, N, 1)
+        out[low : low + CHUNK, :] = jnp.where(half, value, turned)
+        out[high : high + CHUNK, :] = jnp.where(half, turned, value)
+    scatter_lines(out, result)
 
 
 def y_inverse_kernel(lines, table, out):
-    gathered = jnp.concatenate([lines[pl.ds(piece, N, stride=3), :] for piece in range(3)], axis=1)
-    out[...] = line_transform(gathered, table[...], -1.0)
+    out[...] = line_transform(gather_lines(lines), table[...], -1.0)
 
 
 def spectrum_kernel(lines, gains, forward, inverse, out, rows, spec, coeff):
-    gathered = jnp.concatenate([lines[pl.ds(piece, N, stride=3), :] for piece in range(3)], axis=1)
+    half = first_half_lanes()
+    for plane in range(N):
+        prior, following = CHUNK * ((plane - 1) % N), CHUNK * ((plane + 1) % N)
+        out[CHUNK * plane : CHUNK * plane + CHUNK, :] = jnp.where(
+            half, lines[prior : prior + CHUNK, :], lines[following : following + CHUNK, :]
+        )
+    gathered = gather_lines(lines)
     turned = jnp.concatenate([gathered, gathered], axis=0).T
     high, low = split(turned)
     rows[...] = mxu(jnp.concatenate([high, low], axis=1), forward[...])
@@ -252,9 +287,7 @@
                 first_half, low_imag, high_real
             )
     high, low = split(coeff[...])
-    result = mxu_nt(inverse[...], jnp.concatenate([high, high, low], axis=1))
-    for piece in range(3):
-        out[pl.ds(piece, N, stride=3), :] = result[:, 128 * piece : 128 * piece + 128]
+    scatter_lines(out, mxu_nt(inverse[...], jnp.concatenate([high, high, low], axis=1)))
 
 
 def final_kernel(chunks, offsets, near, table, out, lines):
@@ -306,12 +339,16 @@
         out[2, 0, :, where] = near[2, :, where] - value[1]
 
 
-def near_kernel(before, own, after, out, planes):
-    for plane, ref in enumerate((before, own, after)):
-        planes[plane] = ref[...]
+def near_kernel(lines, own, out, planes):
+    half = first_half_lanes()
+    planes[1] = own[...]
+    for tile, start, low, high in pieces():
+        left, right = lines[low : low + CHUNK, :], lines[high : high + CHUNK, :]
+        planes[0, tile, start : start + CHUNK, :] = jnp.where(half, left, pltpu.roll(right, N, 1))
+        planes[2, tile, start : start + CHUNK, :] = jnp.where(half, pltpu.roll(left, N, 1), right)
     first_half = lax.broadcasted_iota(jnp.int32, (8, 128), 1) < N
     targets = [
-        [own[k, pl.ds(4 + comp, 8, stride=4), :] for k in range(4)]
+        [own[k, pl.ds(FIRST_OWN + comp, 8, stride=4), :] for k in range(4)]
         for comp in range(3)
     ]
 
@@ -320,7 +357,7 @@
         for shift_y in (-1, 0, 1):
             for pair in range(4):
                 window = [
-                    planes[plane, pair, pl.ds(4 + 4 * shift_y + comp, 8, stride=4), :]
+                    planes[plane, pair, pl.ds(FIRST_OWN + 4 * shift_y + comp, 8, stride=4), :]
                     for comp in range(4)
                 ]
                 window[0] = window[0] + (plane - 1).astype(jnp.float32)
@@ -377,15 +414,10 @@
     return pltpu.with_memory_space_constraint(jnp.asarray(value), pltpu.HBM)
 
 
-def shift_axis(value, axis, step):
-    count = lax.axis_size(axis)
-    return lax.ppermute(value, axis, [(i, (i + step) % count) for i in range(count)])
-
-
 def exchange_rows(value, axis):
-    rows = value.reshape(64, 1, LANES)
+    rows = value.reshape(N, CHUNK, 128)
     rows = lax.all_to_all(rows, axis, split_axis=0, concat_axis=0, tiled=True)
-    return rows.reshape(192, 128)
+    return rows.reshape(N * CHUNK, 128)
 
 
 def stages(offsets, masses, kernel):
@@ -414,14 +446,12 @@
     chunks, gains = lax.optimization_barrier((chunks, gains))
     chunks = lax.all_to_all(chunks, "gy", split_axis=0, concat_axis=0, tiled=True)
     lines, extended = call(
-        y_forward_kernel, (shape(192, 128), shape(4, ROWS, 128)), [], 1000
+        y_forward_kernel, (shape(N * CHUNK, 128), shape(4, ROWS, 128)), [], 1000
     )(chunks, packed, left)
     lines = exchange_rows(lines, "gx")
-    before = shift_axis(extended, "gx", 1)
-    after = shift_axis(extended, "gx", -1)
     lines = call(
         spectrum_kernel,
-        shape(192, 128),
+        shape(N * CHUNK, 128),
         [
             VMEM((LANES, 128), jnp.float32),
             VMEM((2, MOMENTS, LANES), jnp.float32),
@@ -431,7 +461,7 @@
     )(lines, gains, jnp.asarray(table_x_forward()), jnp.asarray(table_x_inverse()))
     lines = exchange_rows(lines, "gx")
     near = call(near_kernel, shape(3, 8, 512), [VMEM((3, 4, ROWS, 128), jnp.float32)], 6000)(
-        before, extended, after
+        lines, extended
     )
     lines = call(y_inverse_kernel, shape(N, LANES), [], 1000)(lines, left)
     chunks = lax.all_to_all(

time: 96.2 us -> 84.5 us (0.88); the launches traced: 94.3 us -> 84.2 us
  waiting for transfers between devices: 11.7 us -> 2.13 us
  starting transfers between devices: 12.2 us -> 7.07 us
  blocking collectives: 59.3 us -> 63.8 us
    ppermute x2 -> x0, waiting for transfers between devices: 11.7 us -> none  [shift_axis(): lax.ppermute(value, axis, [(i, (i + step) % count) for i in range(count)])]
    ppermute x2 -> x0, starting transfers between devices: 5.28 us -> none  [shift_axis(): lax.ppermute(value, axis, [(i, (i + step) % count) for i in range(count)])]
    all_to_all x2, blocking collectives: 44 us -> 48.5 us  [exchange_rows(): rows = lax.all_to_all(rows, axis, split_axis=0, concat_axis=0, tiled=True)]
    all_to_all x1, waiting for transfers between devices: 0.01 us -> 2.13 us  [stages(): lax.all_to_all(lines.reshape(8, 8, LANES), 'gy', split_axis=0, concat_axi...]
  transfers between devices with their start and end apart: 3 -> 1, of which waited for: 2 -> 1; matrix products, arithmetic and copies ran while one was open for 0% -> 0% of each run, Pallas kernels for 3% -> 4%
where the time goes in v3:
time: 84.5 us; the launch traced here: 84.2 us
  blocking collectives  63.8 us (76%)
  Pallas kernels  9.2 us (11%)
  starting transfers between devices  7.07 us (8%)
  waiting for transfers between devices  2.13 us (3%)
  local copies, waits for them, and re-layouts  1.9 us (2%)
    all_to_all x2, blocking collectives, exchange_rows(): rows = lax.all_to_all(rows, axis, split_axis=0, concat_axis=0, tiled=True)  48.5 us
    all_to_all x1, blocking collectives, stages(): lax.all_to_all(chunks, 'gy', split_axis=0, concat_axis=0, tiled=True)  15.3 us
    all_to_all x1, starting transfers between devices, stages(): lax.all_to_all(lines.reshape(8, 8, LANES), 'gy', split_axis=0, concat_axi...  7.07 us
    pallas_call x1, Pallas kernels, stages(): call(near_kernel, shape(3, 8, 512), [VMEM((3, 4, ROWS, 128), jnp.float32)...  3.22 us
    all_to_all x1, waiting for transfers between devices, stages(): lax.all_to_all(lines.reshape(8, 8, LANES), 'gy', split_axis=0, concat_axi...  2.13 us
    pallas_call x1, Pallas kernels, stages(): call(spectrum_kernel, shape(N * CHUNK, 128), [VMEM((LANES, 128), jnp.floa...  2.07 us
  transfers between devices with their start and end apart: 1, of which 1 were waited for; matrix products, arithmetic and copies ran while one was open for 0% of the time, Pallas kernels for 4%

profile of v3, /device:TPU:1, one launch (start us, length us, event | category | flops | bytes accessed | tf_op | source)
XLA Modules:
  0.0 84.2 jit_solution(15391434205432893138)
XLA Ops:
  0.0 0.0 slice-start
  0.0 1.6 %slice-done = bf16[36,2,36,1,384]{4,1,3,2,0:T(2,128)(2,1)S(1)} async-done(((bf16[36,2,36,1,512]{4,1,3,2,0:T(2,128)(2,1)}), bf16[36,2,36,1,384]{4,1,3,2,0:T(2,128)(2,1)S(1)}, s32[]{:S(2)}) %slice-start) | async-done | bytes 1990680 | tf_op jit(solution)/shard_map/slice | solution.py:426
  1.6 0.0 copy-start.2
  1.6 0.0 copy-start.3
  1.6 0.3 copy.12
  1.9 1.5 %shard_map.82 = (f32[8,8,640]{2,1,0:T(8,128)S(1)}, f32[4,32,128]{2,1,0:T(8,128)S(1)}, bf16[128,192]{1,0:T(8,128)(2,1)S(1)}) custom-call(f32[3,1,8,512]{3,2,1,0:T(8,128)} %offsets.1, f32[1,8,512]{2,1,0:T(8,128)} %masses_hbm.1, bf16[256,128]{1,0:T(8,128)(2,1)} %constant.10.clone.table_hbm, bf16[128,192]{1,0:T(8,128)(2,1)} %constant.11.clone.left_hbm), custom_call_target="tpu_custom_call" | custom-call | flops 2000000 | bytes 2000 | tf_op jit(solution)/shard_map/pallas_call | solution.py:427
  3.4 15.3 %all_to_all.20.chunks = f32[8,8,640]{2,1,0:T(8,128)S(1)} all-to-all(f32[8,8,640]{2,1,0:T(8,128)S(1)} %get-tuple-element.17), channel_id=1, replica_groups=mesh['gx'=64,'gy'=8] {'gy'}, dimensions={0} | all-to-all | bytes 327680 | tf_op jit(solution)/shard_map/all_to_all | solution.py:447
  18.7 0.3 shard_map.83
  19.0 27.3 %all_to_all.21 = f32[64,8,128]{2,1,0:T(8,128)S(1)} all-to-all(f32[64,8,128]{2,1,0:T(8,128)S(1)} %bitcast.14), channel_id=1, replica_groups=mesh['gx'=64,'gy'=8] {'gx'}, dimensions={0} | all-to-all | bytes 524288 | tf_op jit(solution)/shard_map/all_to_all | solution.py:419
  46.3 0.0 copy-start
  46.3 0.0 copy-start.1
  46.3 0.0 copy-done.2
  46.3 0.0 copy-done.3
  46.3 2.1 %shard_map.84 = f32[512,128]{1,0:T(8,128)S(1)} custom-call(f32[512,128]{1,0:T(8,128)S(1)} %bitcast.12, bf16[36,2,36,384]{3,2,1,0:T(8,128)(2,1)S(1)} %bitcast.9, bf16[256,128]{1,0:T(8,128)(2,1)S(1)} %copy-done.2, bf16[64,384]{1,0:T(8,128)(2,1)S(1)} %copy-done.3), custom_call_target="tpu_custom_call" | custom-call | flops 3000000 | bytes 3000 | tf_op jit(solution)/shard_map/pallas_call | solution.py:452
  48.4 21.2 %all_to_all.22 = f32[64,8,128]{2,1,0:T(8,128)S(1)} all-to-all(f32[64,8,128]{2,1,0:T(8,128)S(1)} %bitcast.13), channel_id=1, replica_groups=mesh['gx'=64,'gy'=8] {'gx'}, dimensions={0} | all-to-all | bytes 524288 | tf_op jit(solution)/shard_map/all_to_all | solution.py:419
  69.6 0.9 %shard_map.85 = f32[64,384]{1,0:T(8,128)} custom-call(f32[512,128]{1,0:T(8,128)S(1)} %bitcast.10, bf16[128,192]{1,0:T(8,128)(2,1)S(1)} %get-tuple-element.19.table), custom_call_target="tpu_custom_call" | custom-call | flops 1000000 | bytes 1000 | tf_op jit(solution)/shard_map/pallas_call | solution.py:466
  70.5 7.1 %all-to-all-start.3 = ((f32[8,8,384]{2,1,0:T(8,128)}), f32[8,8,384]{2,1,0:T(8,128)S(1)}, u32[]{:S(2)}, u32[]{:S(2)}) async-start(f32[8,8,384]{2,1,0:T(8,128)} %bitcast.6), calls=%async_computation.3 | async-start | bytes 196608 | tf_op jit(solution)/shard_map/all_to_all | solution.py:467
  77.6 3.2 %shard_map.86.near = f32[3,8,512]{2,1,0:T(8,128)S(1)} custom-call(f32[512,128]{1,0:T(8,128)S(1)} %bitcast.11, f32[4,48,128]{2,1,0:T(8,128)S(1)} %get-tuple-element.22.own), custom_call_target="tpu_custom_call" | custom-call | flops 6000000 | bytes 6000 | tf_op jit(solution)/shard_map/pallas_call | solution.py:463
  80.8 2.1 %all-to-all-done.3.chunks = f32[8,8,384]{2,1,0:T(8,128)S(1)} async-done(((f32[8,8,384]{2,1,0:T(8,128)}), f32[8,8,384]{2,1,0:T(8,128)S(1)}, u32[]{:S(2)}, u32[]{:S(2)}) %all-to-all-start.3) | async-done | bytes 98336 | tf_op jit(solution)/shard_map/all_to_all | solution.py:467
  83.0 0.0 copy-done
  83.0 0.0 copy-done.1
  83.0 1.2 %shard_map.87 = f32[3,1,8,512]{3,2,1,0:T(8,128)} custom-call(f32[8,8,384]{2,1,0:T(8,128)S(1)} %all-to-all-done.3.chunks, f32[3,1,8,512]{3,2,1,0:T(8,128)S(1)} %copy-done, f32[3,8,512]{2,1,0:T(8,128)S(1)} %shard_map.86.near, bf16[384,128]{1,0:T(8,128)(2,1)S(1)} %copy-done.1), custom_call_target="tpu_custom_call" | custom-call | flops 2000000 | bytes 2000 | tf_op jit(solution)/shard_map/pallas_call | solution.py:470
Async XLA Ops:
  0.0 1.6 %slice-start = ((bf16[36,2,36,1,512]{4,1,3,2,0:T(2,128)(2,1)}), bf16[36,2,36,1,384]{4,1,3,2,0:T(2,128)(2,1)S(1)}, s32[]{:S(2)}) async-start(bf16[36,2,36,1,512]{4,1,3,2,0:T(2,128)(2,1)} %param.10), calls=%async_computation.4 | async-start | bytes 3981312 | tf_op jit(solution)/shard_map/slice | solution.py:426
  1.6 44.7 %copy-start.2 = (bf16[256,128]{1,0:T(8,128)(2,1)S(1)}, bf16[256,128]{1,0:T(8,128)(2,1)}, u32[]{:S(2)}) copy-start(bf16[256,128]{1,0:T(8,128)(2,1)} %constant.12.clone.forward) | copy-start | bytes 196612
  1.6 44.7 %copy-start.3 = (bf16[64,384]{1,0:T(8,128)(2,1)S(1)}, bf16[64,384]{1,0:T(8,128)(2,1)}, u32[]{:S(2)}) copy-start(bf16[64,384]{1,0:T(8,128)(2,1)} %constant.13.clone.inverse) | copy-start | bytes 147460
  46.3 36.7 %copy-start = (f32[3,1,8,512]{3,2,1,0:T(8,128)S(1)}, f32[3,1,8,512]{3,2,1,0:T(8,128)}, u32[]{:S(2)}) copy-start(f32[3,1,8,512]{3,2,1,0:T(8,128)} %offsets.1) | copy-start | bytes 147460
  46.3 36.7 %copy-start.1 = (bf16[384,128]{1,0:T(8,128)(2,1)S(1)}, bf16[384,128]{1,0:T(8,128)(2,1)}, u32[]{:S(2)}) copy-start(bf16[384,128]{1,0:T(8,128)(2,1)} %constant.14.clone.table) | copy-start | bytes 294916
  70.5 12.4 %all-to-all-start.3 = ((f32[8,8,384]{2,1,0:T(8,128)}), f32[8,8,384]{2,1,0:T(8,128)S(1)}, u32[]{:S(2)}, u32[]{:S(2)}) async-start(f32[8,8,384]{2,1,0:T(8,128)} %bitcast.6), calls=%async_computation.3 | async-start | bytes 196608 | tf_op jit(solution)/shard_map/all_to_all | solution.py:467

commit v4 on v2

--- a/solution.py
+++ b/solution.py
@@ -101,7 +101,11 @@
 
 
 EDGE = 256
-ROWS = 4 * 10
+LEAD = 3
+TILE_ROWS = 40
+PIECES = 54
+FLAT = 168
+FORWARD, INVERSE = 6, 9
 
 
 def edge_places(comp):
@@ -116,9 +120,11 @@
     masses_hbm,
     table_hbm,
     left_hbm,
+    gains_hbm,
     chunks,
     packed,
     left,
+    gains,
     offsets,
     masses,
     table,
@@ -130,6 +136,10 @@
         (masses_hbm, masses),
         (table_hbm, table),
         (left_hbm, left),
+    )
+    pairs += tuple(
+        (gains_hbm.at[row, :, :, pl.ds(0, LANES)], gains.at[:, pl.ds(2 * row, 2), :])
+        for row in range(MOMENTS)
     )
     copies = [pltpu.make_async_copy(a, b, sems.at[i]) for i, (a, b) in enumerate(pairs)]
     for copy in copies:
@@ -169,7 +179,8 @@
             chunks[block, :, channel * GROUP : (channel + 1) * GROUP] = rows[
                 :, block * GROUP : (block + 1) * GROUP
             ]
-    copies[3].wait()
+    for copy in copies[3:]:
+        copy.wait()
 
 
 def line_transform(lines, table, direction):
@@ -185,27 +196,50 @@
     return cos_part + swapped * factor
 
 
+def gather_lines(lines, chunk):
+    return jnp.concatenate([lines[pl.ds(row, N, stride=chunk), :] for row in range(LEAD)], axis=1)
+
+
+def scatter_lines(out, result, chunk):
+    for row in range(LEAD):
+        out[pl.ds(row, N, stride=chunk), :] = result[:, 128 * row : 128 * row + 128]
+
+
 def y_forward_kernel(chunks, packed, table, out, extended):
-    result = line_transform(chunks[:, :, :LANES].reshape(N, LANES), table[...], 1.0)
-    for piece in range(3):
-        out[pl.ds(piece, N, stride=3), :] = result[:, 128 * piece : 128 * piece + 128]
     me = lax.axis_index("gy")
     after, before = lax.rem(me + 1, 8), lax.rem(me + 7, 8)
-    extended[:, 4 : ROWS - 4, :] = packed[...]
+    extended[4 * TILE_ROWS :, :] = jnp.zeros((FLAT - 4 * TILE_ROWS, 128), jnp.float32)
+    out[...] = jnp.zeros_like(out)
+    for tile in range(4):
+        first = TILE_ROWS * tile
+        extended[first + 4 : first + 36, :] = packed[tile]
     for comp in range(4):
-        last = ROWS - 4 + comp
         for tile, row, lanes in edge_places(comp):
-            extended[tile, comp : comp + 1, :] = chunks[before, row : row + 1, lanes]
-            extended[tile, last : last + 1, :] = chunks[after, row : row + 1, lanes]
+            top = TILE_ROWS * tile + comp
+            extended[top : top + 1, :] = chunks[before, row : row + 1, lanes]
+            extended[top + 36 : top + 37, :] = chunks[after, row : row + 1, lanes]
+    result = line_transform(chunks[:, :, :LANES].reshape(N, LANES), table[...], 1.0)
+    scatter_lines(out, result, FORWARD)
+    for row in range(3):
+        out[pl.ds(LEAD + row, PIECES, stride=FORWARD), :] = extended[pl.ds(row, PIECES, stride=3), :]
 
 
 def y_inverse_kernel(lines, table, out):
-    gathered = jnp.concatenate([lines[pl.ds(piece, N, stride=3), :] for piece in range(3)], axis=1)
-    out[...] = line_transform(gathered, table[...], -1.0)
-
-
-def spectrum_kernel(lines, gains, forward, inverse, out, rows, spec, coeff):
-    gathered = jnp.concatenate([lines[pl.ds(piece, N, stride=3), :] for piece in range(3)], axis=1)
+    out[...] = line_transform(gather_lines(lines, INVERSE), table[...], -1.0)
+
+
+def spectrum_kernel(lines, gains, forward, inverse, out, rows, spec, coeff, sums):
+    for row in range(LEAD, 2 * LEAD):
+        last, other = N - 1, row + LEAD
+        out[pl.ds(INVERSE + row, last, stride=INVERSE), :] = lines[
+            pl.ds(row, last, stride=FORWARD), :
+        ]
+        out[row : row + 1, :] = lines[FORWARD * last + row : FORWARD * last + row + 1, :]
+        out[pl.ds(other, last, stride=INVERSE), :] = lines[
+            pl.ds(FORWARD + row, last, stride=FORWARD), :
+        ]
+        out[INVERSE * last + other : INVERSE * last + other + 1, :] = lines[row : row + 1, :]
+    gathered = gather_lines(lines, FORWARD)
     turned = jnp.concatenate([gathered, gathered], axis=0).T
     high, low = split(turned)
     rows[...] = mxu(jnp.concatenate([high, low], axis=1), forward[...])
@@ -220,26 +254,25 @@
     real_first.append(real_first[-1])
     imag_first.append(imag_first[-1])
     for pair in range(3):
-        where = slice(128 * pair, 128 * pair + 128)
-        spec[0, :, where] = jnp.where(first_half, real_first[2 * pair], imag_first[2 * pair + 1])
-        spec[1, :, where] = jnp.where(first_half, imag_first[2 * pair], real_first[2 * pair + 1])
-
-    def add_channel(channel, running):
-        real_sum, imag_sum = running
-        gain_real = gains[channel, 0].astype(jnp.float32)
-        gain_imag = gains[channel, 1].astype(jnp.float32)
-        spec_real = spec[0, pl.ds(channel, 1), :]
-        spec_imag = spec[1, pl.ds(channel, 1), :]
-        real_sum = real_sum + (gain_real * spec_real - gain_imag * spec_imag)
-        imag_sum = imag_sum + (gain_real * spec_imag + gain_imag * spec_real)
-        return real_sum, imag_sum
-
-    zero = jnp.zeros((MOMENTS, 128 * 3), jnp.float32)
-    real_sum, imag_sum = lax.fori_loop(0, MOMENTS, add_channel, (zero, zero))
+        spec[0, pair] = jnp.where(first_half, real_first[2 * pair], imag_first[2 * pair + 1])
+        spec[1, pair] = jnp.where(first_half, imag_first[2 * pair], real_first[2 * pair + 1])
+
     coeff[...] = jnp.zeros_like(coeff)
     for pair in range(3):
         where = slice(128 * pair, 128 * pair + 128)
-        real_part, imag_part = real_sum[:, where], imag_sum[:, where]
+
+        def add_channel(channel, running):
+            by_real, by_imag = running
+            gain = gains[channel, :, where].astype(jnp.float32)
+            by_real = by_real + gain * spec[0, pair, pl.ds(channel, 1), :]
+            by_imag = by_imag + gain * spec[1, pair, pl.ds(channel, 1), :]
+            return by_real, by_imag
+
+        zero = jnp.zeros((2 * MOMENTS, 128), jnp.float32)
+        sums[0], sums[1] = lax.fori_loop(0, MOMENTS, add_channel, (zero, zero), unroll=4)
+        even, odd = pl.ds(0, MOMENTS, stride=2), pl.ds(1, MOMENTS, stride=2)
+        real_part = sums[0, even, :] - sums[1, odd, :]
+        imag_part = sums[0, odd, :] + sums[1, even, :]
         real_roll, imag_roll = pltpu.roll(real_part, N, 1), pltpu.roll(imag_part, N, 1)
         for half in range(2):
             kz = 2 * pair + half
@@ -252,9 +285,9 @@
                 first_half, low_imag, high_real
             )
     high, low = split(coeff[...])
-    result = mxu_nt(inverse[...], jnp.concatenate([high, high, low], axis=1))
-    for piece in range(3):
-        out[pl.ds(piece, N, stride=3), :] = result[:, 128 * piece : 128 * piece + 128]
+    scatter_lines(
+        out, mxu_nt(inverse[...], jnp.concatenate([high, high, low], axis=1)), INVERSE
+    )
 
 
 def final_kernel(chunks, offsets, near, table, out, lines):
@@ -306,12 +339,16 @@
         out[2, 0, :, where] = near[2, :, where] - value[1]
 
 
-def near_kernel(before, own, after, out, planes):
-    for plane, ref in enumerate((before, own, after)):
-        planes[plane] = ref[...]
+def near_kernel(lines, own, out, planes):
+    planes[1] = own[...]
+    for row in range(3):
+        for plane, lead in ((0, LEAD), (2, 2 * LEAD)):
+            planes[plane, pl.ds(row, PIECES, stride=3), :] = lines[
+                pl.ds(lead + row, PIECES, stride=INVERSE), :
+            ]
     first_half = lax.broadcasted_iota(jnp.int32, (8, 128), 1) < N
     targets = [
-        [own[k, pl.ds(4 + comp, 8, stride=4), :] for k in range(4)]
+        [own[pl.ds(TILE_ROWS * k + 4 + comp, 8, stride=4), :] for k in range(4)]
         for comp in range(3)
     ]
 
@@ -320,7 +357,11 @@
         for shift_y in (-1, 0, 1):
             for pair in range(4):
                 window = [
-                    planes[plane, pair, pl.ds(4 + 4 * shift_y + comp, 8, stride=4), :]
+                    planes[
+                        plane,
+                        pl.ds(TILE_ROWS * pair + 4 + 4 * shift_y + comp, 8, stride=4),
+                        :,
+                    ]
                     for comp in range(4)
                 ]
                 window[0] = window[0] + (plane - 1).astype(jnp.float32)
@@ -377,61 +418,53 @@
     return pltpu.with_memory_space_constraint(jnp.asarray(value), pltpu.HBM)
 
 
-def shift_axis(value, axis, step):
-    count = lax.axis_size(axis)
-    return lax.ppermute(value, axis, [(i, (i + step) % count) for i in range(count)])
-
-
 def exchange_rows(value, axis):
-    rows = value.reshape(64, 1, LANES)
+    rows = value.reshape(N, 1, -1)
     rows = lax.all_to_all(rows, axis, split_axis=0, concat_axis=0, tiled=True)
-    return rows.reshape(192, 128)
+    return rows.reshape(value.shape)
 
 
 def stages(offsets, masses, kernel):
     hbm = pl.BlockSpec(memory_space=pltpu.HBM)
     table_z, table_y = table_z_forward(), table_left()
-    gains = kernel[:, :, :, 0, :LANES]
-    chunks, packed, left = call(
+    gains = jnp.transpose(kernel[:, :, :, 0, :], (0, 2, 1, 3))
+    chunks, packed, left, gains = call(
         moments_kernel,
         (
             shape(8, 8, LANES + EDGE),
             shape(4, 32, 128),
             shape(*table_y.shape, dtype=jnp.bfloat16),
+            shape(MOMENTS, 2 * MOMENTS, LANES, dtype=jnp.bfloat16),
         ),
         [
             VMEM((3, 1, 8, 512), jnp.float32),
             VMEM((1, 8, 512), jnp.float32),
             VMEM(table_z.shape, jnp.bfloat16),
             VMEM((8 * MOMENTS, 128), jnp.float32),
-            pltpu.SemaphoreType.DMA((4,)),
+            pltpu.SemaphoreType.DMA((4 + MOMENTS,)),
         ],
         2000,
-        [hbm] * 4,
-    )(*(far_memory(value) for value in (offsets, masses, table_z, table_y)))
-    chunks, gains = lax.optimization_barrier((chunks, gains))
-    gains = jnp.transpose(gains, (2, 1, 0, 3))
-    chunks, gains = lax.optimization_barrier((chunks, gains))
+        [hbm] * 5,
+    )(*(far_memory(value) for value in (offsets, masses, table_z, table_y, gains)))
     chunks = lax.all_to_all(chunks, "gy", split_axis=0, concat_axis=0, tiled=True)
     lines, extended = call(
-        y_forward_kernel, (shape(192, 128), shape(4, ROWS, 128)), [], 1000
+        y_forward_kernel, (shape(N * FORWARD, 128), shape(FLAT, 128)), [], 1000
     )(chunks, packed, left)
     lines = exchange_rows(lines, "gx")
-    before = shift_axis(extended, "gx", 1)
-    after = shift_axis(extended, "gx", -1)
     lines = call(
         spectrum_kernel,
-        shape(192, 128),
+        shape(N * INVERSE, 128),
         [
             VMEM((LANES, 128), jnp.float32),
-            VMEM((2, MOMENTS, LANES), jnp.float32),
+            VMEM((2, 3, MOMENTS, 128), jnp.float32),
             VMEM((LANES, 128), jnp.float32),
+            VMEM((2, 2 * MOMENTS, 128), jnp.float32),
         ],
         3000,
     )(lines, gains, jnp.asarray(table_x_forward()), jnp.asarray(table_x_inverse()))
     lines = exchange_rows(lines, "gx")
-    near = call(near_kernel, shape(3, 8, 512), [VMEM((3, 4, ROWS, 128), jnp.float32)], 6000)(
-        before, extended, after
+    near = call(near_kernel, shape(3, 8, 512), [VMEM((3, FLAT, 128), jnp.float32)], 6000)(
+        lines, extended
     )
     lines = call(y_inverse_kernel, shape(N, LANES), [], 1000)(lines, left)
     chunks = lax.all_to_all(

time: 96.2 us -> 82 us (0.85); the launches traced: 94.3 us -> 81.6 us
  waiting for transfers between devices: 11.7 us -> 2.24 us
  starting transfers between devices: 12.2 us -> 7.59 us
  blocking collectives: 59.3 us -> 62.5 us
  local copies, waits for them, and re-layouts: 1.9 us -> 0.02 us
    ppermute x2 -> x0, waiting for transfers between devices: 11.7 us -> none  [shift_axis(): lax.ppermute(value, axis, [(i, (i + step) % count) for i in range(count)])]
    ppermute x2 -> x0, starting transfers between devices: 5.28 us -> none  [shift_axis(): lax.ppermute(value, axis, [(i, (i + step) % count) for i in range(count)])]
    all_to_all x2, blocking collectives: 44 us -> 47.1 us  [exchange_rows(): rows = lax.all_to_all(rows, axis, split_axis=0, concat_axis=0, tiled=True)]
    all_to_all x1, waiting for transfers between devices: 0.01 us -> 2.24 us  [stages(): lax.all_to_all(lines.reshape(8, 8, LANES), 'gy', split_axis=0, concat_axi...]
    slice x2 -> x0, local copies, waits for them, and re-layouts: 1.55 us -> none  [stages(): gains = kernel[:, :, :, 0, :LANES]]
  transfers between devices with their start and end apart: 3 -> 1, of which waited for: 2 -> 1; matrix products, arithmetic and copies ran while one was open for 0% -> 0% of each run, Pallas kernels for 3% -> 4%
where the time goes in v4:
time: 82 us; the launch traced here: 81.6 us
  blocking collectives  62.5 us (76%)
  Pallas kernels  9.22 us (11%)
  starting transfers between devices  7.59 us (9%)
  waiting for transfers between devices  2.24 us (3%)
    all_to_all x2, blocking collectives, exchange_rows(): rows = lax.all_to_all(rows, axis, split_axis=0, concat_axis=0, tiled=True)  47.1 us
    all_to_all x1, blocking collectives, stages(): lax.all_to_all(chunks, 'gy', split_axis=0, concat_axis=0, tiled=True)  15.4 us
    all_to_all x1, starting transfers between devices, stages(): lax.all_to_all(lines.reshape(8, 8, LANES), 'gy', split_axis=0, concat_axi...  7.59 us
    pallas_call x1, Pallas kernels, stages(): call(near_kernel, shape(3, 8, 512), [VMEM((3, FLAT, 128), jnp.float32)],...  3.11 us
    all_to_all x1, waiting for transfers between devices, stages(): lax.all_to_all(lines.reshape(8, 8, LANES), 'gy', split_axis=0, concat_axi...  2.24 us
    pallas_call x1, Pallas kernels, stages(): call(moments_kernel, (shape(8, 8, LANES + EDGE), shape(4, 32, 128), shape...  1.97 us
    pallas_call x1, Pallas kernels, stages(): call(spectrum_kernel, shape(N * INVERSE, 128), [VMEM((LANES, 128), jnp.fl...  1.72 us
  transfers between devices with their start and end apart: 1, of which 1 were waited for; matrix products, arithmetic and copies ran while one was open for 0% of the time, Pallas kernels for 4%

profile of v4, /device:TPU:1, one launch (start us, length us, event | category | flops | bytes accessed | tf_op | source)
XLA Modules:
  0.0 81.6 jit_solution(298338844617878918)
XLA Ops:
  0.0 0.0 copy-start.3
  0.0 0.0 copy-start.2
  0.0 2.0 %shard_map.82 = (f32[8,8,640]{2,1,0:T(8,128)S(1)}, f32[4,32,128]{2,1,0:T(8,128)S(1)}, bf16[128,192]{1,0:T(8,128)(2,1)S(1)}, bf16[36,72,384]{2,1,0:T(8,128)(2,1)S(1)}) custom-call(f32[3,1,8,512]{3,2,1,0:T(8,128)} %offsets.1, f32[1,8,512]{2,1,0:T(8,128)} %masses_hbm.1, bf16[256,128]{1,0:T(8,128)(2,1)} %constant.10.clone.table_hbm, ...), custom_call_target="tpu_custom_call" | custom-call | flops 2000000 | bytes 2000 | tf_op jit(solution)/shard_map/pallas_call | solution.py:431
  2.0 0.0 copy-start
  2.0 0.0 copy-start.1
  2.0 15.4 %all_to_all.20.chunks = f32[8,8,640]{2,1,0:T(8,128)S(1)} all-to-all(f32[8,8,640]{2,1,0:T(8,128)S(1)} %get-tuple-element.11), channel_id=1, replica_groups=mesh['gx'=64,'gy'=8] {'gy'}, dimensions={0} | all-to-all | bytes 327680 | tf_op jit(solution)/shard_map/all_to_all | solution.py:449
  17.4 0.3 shard_map.83
  17.7 27.1 %all_to_all.21 = f32[64,1,768]{2,1,0:T(1,128)S(1)} all-to-all(f32[64,1,768]{2,1,0:T(1,128)S(1)} %bitcast.12), channel_id=1, replica_groups=mesh['gx'=64,'gy'=8] {'gx'}, dimensions={0} | all-to-all | bytes 393216 | tf_op jit(solution)/shard_map/all_to_all | solution.py:423
  44.8 0.0 copy-done.3
  44.8 0.0 copy-done.2
  44.8 1.7 %shard_map.84 = f32[576,128]{1,0:T(8,128)S(1)} custom-call(f32[384,128]{1,0:T(8,128)S(1)} %bitcast.11, bf16[36,72,384]{2,1,0:T(8,128)(2,1)S(1)} %get-tuple-element.15.gains, bf16[256,128]{1,0:T(8,128)(2,1)S(1)} %copy-done.2, bf16[64,384]{1,0:T(8,128)(2,1)S(1)} %copy-done.3), custom_call_target="tpu_custom_call" | custom-call | flops 3000000 | bytes 3000 | tf_op jit(solution)/shard_map/pallas_call | solution.py:454
  46.6 20.0 %all_to_all.22 = f32[64,1,1152]{2,1,0:T(1,128)S(1)} all-to-all(f32[64,1,1152]{2,1,0:T(1,128)S(1)} %bitcast.10), channel_id=1, replica_groups=mesh['gx'=64,'gy'=8] {'gx'}, dimensions={0} | all-to-all | bytes 589824 | tf_op jit(solution)/shard_map/all_to_all | solution.py:423
  66.5 0.9 %shard_map.85 = f32[64,384]{1,0:T(8,128)} custom-call(f32[576,128]{1,0:T(8,128)S(1)} %bitcast.8, bf16[128,192]{1,0:T(8,128)(2,1)S(1)} %get-tuple-element.13.table), custom_call_target="tpu_custom_call" | custom-call | flops 1000000 | bytes 1000 | tf_op jit(solution)/shard_map/pallas_call | solution.py:469
  67.5 7.6 %all-to-all-start.3 = ((f32[8,8,384]{2,1,0:T(8,128)}), f32[8,8,384]{2,1,0:T(8,128)S(1)}, u32[]{:S(2)}, u32[]{:S(2)}) async-start(f32[8,8,384]{2,1,0:T(8,128)} %bitcast.6), calls=%async_computation.3 | async-start | bytes 196608 | tf_op jit(solution)/shard_map/all_to_all | solution.py:470
  75.1 3.1 %shard_map.86.near = f32[3,8,512]{2,1,0:T(8,128)S(1)} custom-call(f32[576,128]{1,0:T(8,128)S(1)} %bitcast.9, f32[168,128]{1,0:T(8,128)S(1)} %get-tuple-element.16.own), custom_call_target="tpu_custom_call" | custom-call | flops 6000000 | bytes 6000 | tf_op jit(solution)/shard_map/pallas_call | solution.py:466
  78.2 2.2 %all-to-all-done.3.chunks = f32[8,8,384]{2,1,0:T(8,128)S(1)} async-done(((f32[8,8,384]{2,1,0:T(8,128)}), f32[8,8,384]{2,1,0:T(8,128)S(1)}, u32[]{:S(2)}, u32[]{:S(2)}) %all-to-all-start.3) | async-done | bytes 98336 | tf_op jit(solution)/shard_map/all_to_all | solution.py:470
  80.4 0.0 copy-done
  80.4 0.0 copy-done.1
  80.4 1.2 %shard_map.87 = f32[3,1,8,512]{3,2,1,0:T(8,128)} custom-call(f32[8,8,384]{2,1,0:T(8,128)S(1)} %all-to-all-done.3.chunks, f32[3,1,8,512]{3,2,1,0:T(8,128)S(1)} %copy-done, f32[3,8,512]{2,1,0:T(8,128)S(1)} %shard_map.86.near, bf16[384,128]{1,0:T(8,128)(2,1)S(1)} %copy-done.1), custom_call_target="tpu_custom_call" | custom-call | flops 2000000 | bytes 2000 | tf_op jit(solution)/shard_map/pallas_call | solution.py:473
Async XLA Ops:
  0.0 44.8 %copy-start.3 = (bf16[64,384]{1,0:T(8,128)(2,1)S(1)}, bf16[64,384]{1,0:T(8,128)(2,1)}, u32[]{:S(2)}) copy-start(bf16[64,384]{1,0:T(8,128)(2,1)} %constant.13.clone.inverse) | copy-start | bytes 147460
  0.0 44.8 %copy-start.2 = (bf16[256,128]{1,0:T(8,128)(2,1)S(1)}, bf16[256,128]{1,0:T(8,128)(2,1)}, u32[]{:S(2)}) copy-start(bf16[256,128]{1,0:T(8,128)(2,1)} %constant.12.clone.forward) | copy-start | bytes 196612
  2.0 78.4 %copy-start = (f32[3,1,8,512]{3,2,1,0:T(8,128)S(1)}, f32[3,1,8,512]{3,2,1,0:T(8,128)}, u32[]{:S(2)}) copy-start(f32[3,1,8,512]{3,2,1,0:T(8,128)} %offsets.1) | copy-start | bytes 147460
  2.0 78.4 %copy-start.1 = (bf16[384,128]{1,0:T(8,128)(2,1)S(1)}, bf16[384,128]{1,0:T(8,128)(2,1)}, u32[]{:S(2)}) copy-start(bf16[384,128]{1,0:T(8,128)(2,1)} %constant.14.clone.table) | copy-start | bytes 294916
  67.5 12.9 %all-to-all-start.3 = ((f32[8,8,384]{2,1,0:T(8,128)}), f32[8,8,384]{2,1,0:T(8,128)S(1)}, u32[]{:S(2)}, u32[]{:S(2)}) async-start(f32[8,8,384]{2,1,0:T(8,128)} %bitcast.6), calls=%async_computation.3 | async-start | bytes 196608 | tf_op jit(solution)/shard_map/all_to_all | solution.py:470

commit v5 on v4

--- a/solution.py
+++ b/solution.py
@@ -103,9 +103,8 @@
 EDGE = 256
 LEAD = 3
 TILE_ROWS = 40
-PIECES = 54
-FLAT = 168
-FORWARD, INVERSE = 6, 9
+FLAT = 160
+FORWARD, INVERSE = 6, 8
 
 
 def edge_places(comp):
@@ -208,8 +207,6 @@
 def y_forward_kernel(chunks, packed, table, out, extended):
     me = lax.axis_index("gy")
     after, before = lax.rem(me + 1, 8), lax.rem(me + 7, 8)
-    extended[4 * TILE_ROWS :, :] = jnp.zeros((FLAT - 4 * TILE_ROWS, 128), jnp.float32)
-    out[...] = jnp.zeros_like(out)
     for tile in range(4):
         first = TILE_ROWS * tile
         extended[first + 4 : first + 36, :] = packed[tile]
@@ -220,8 +217,11 @@
             extended[top + 36 : top + 37, :] = chunks[after, row : row + 1, lanes]
     result = line_transform(chunks[:, :, :LANES].reshape(N, LANES), table[...], 1.0)
     scatter_lines(out, result, FORWARD)
-    for row in range(3):
-        out[pl.ds(LEAD + row, PIECES, stride=FORWARD), :] = extended[pl.ds(row, PIECES, stride=3), :]
+    for row in range(2):
+        out[pl.ds(LEAD + row, N, stride=FORWARD), :] = extended[pl.ds(row, N, stride=2), :]
+    tail = extended[2 * N :, :]
+    out[pl.ds(LEAD + 2, N // 2, stride=FORWARD), :] = tail
+    out[pl.ds(FORWARD * N // 2 + LEAD + 2, N // 2, stride=FORWARD), :] = pltpu.roll(tail, N, 1)
 
 
 def y_inverse_kernel(lines, table, out):
@@ -229,16 +229,22 @@
 
 
 def spectrum_kernel(lines, gains, forward, inverse, out, rows, spec, coeff, sums):
+    half = lax.broadcasted_iota(jnp.int32, (1, 128), 1) < N
+
+    def relay(row, start, count, prior, following):
+        ahead = lines[pl.ds(FORWARD * prior + row, count, stride=FORWARD), :]
+        behind = lines[pl.ds(FORWARD * following + row, count, stride=FORWARD), :]
+        first = INVERSE * start + 2 * row - LEAD
+        rows = pl.ds(first, count, stride=INVERSE)
+        out[rows, :] = jnp.where(half, ahead, pltpu.roll(behind, N, 1))
+        if row < 2 * LEAD - 1:
+            rows = pl.ds(first + 1, count, stride=INVERSE)
+            out[rows, :] = jnp.where(half, pltpu.roll(ahead, N, 1), behind)
+
     for row in range(LEAD, 2 * LEAD):
-        last, other = N - 1, row + LEAD
-        out[pl.ds(INVERSE + row, last, stride=INVERSE), :] = lines[
-            pl.ds(row, last, stride=FORWARD), :
-        ]
-        out[row : row + 1, :] = lines[FORWARD * last + row : FORWARD * last + row + 1, :]
-        out[pl.ds(other, last, stride=INVERSE), :] = lines[
-            pl.ds(FORWARD + row, last, stride=FORWARD), :
-        ]
-        out[INVERSE * last + other : INVERSE * last + other + 1, :] = lines[row : row + 1, :]
+        relay(row, 1, N - 2, 0, 2)
+        relay(row, 0, 1, N - 1, 1)
+        relay(row, N - 1, 1, N - 2, 0)
     gathered = gather_lines(lines, FORWARD)
     turned = jnp.concatenate([gathered, gathered], axis=0).T
     high, low = split(turned)
@@ -341,11 +347,22 @@
 
 def near_kernel(lines, own, out, planes):
     planes[1] = own[...]
-    for row in range(3):
-        for plane, lead in ((0, LEAD), (2, 2 * LEAD)):
-            planes[plane, pl.ds(row, PIECES, stride=3), :] = lines[
-                pl.ds(lead + row, PIECES, stride=INVERSE), :
-            ]
+    half = lax.broadcasted_iota(jnp.int32, (1, 128), 1) < N
+
+    def unpack(rows, low, high):
+        planes[0, rows, :] = jnp.where(half, low, pltpu.roll(high, N, 1))
+        planes[2, rows, :] = jnp.where(half, pltpu.roll(low, N, 1), high)
+
+    for row in range(2):
+        low, high = (
+            lines[pl.ds(LEAD + 2 * row + side, N, stride=INVERSE), :] for side in range(2)
+        )
+        unpack(pl.ds(row, N, stride=2), low, high)
+    low, high = (
+        lines[pl.ds(INVERSE * N // 2 * side + INVERSE - 1, N // 2, stride=INVERSE), :]
+        for side in range(2)
+    )
+    unpack(pl.ds(2 * N, N // 2), low, high)
     first_half = lax.broadcasted_iota(jnp.int32, (8, 128), 1) < N
     targets = [
         [own[pl.ds(TILE_ROWS * k + 4 + comp, 8, stride=4), :] for k in range(4)]
@@ -419,7 +436,7 @@
 
 
 def exchange_rows(value, axis):
-    rows = value.reshape(N, 1, -1)
+    rows = value.reshape((N, 8, 128) if value.shape[0] == 8 * N else (N, 1, -1))
     rows = lax.all_to_all(rows, axis, split_axis=0, concat_axis=0, tiled=True)
     return rows.reshape(value.shape)
 
@@ -427,7 +444,7 @@
 def stages(offsets, masses, kernel):
     hbm = pl.BlockSpec(memory_space=pltpu.HBM)
     table_z, table_y = table_z_forward(), table_left()
-    gains = jnp.transpose(kernel[:, :, :, 0, :], (0, 2, 1, 3))
+    matrices = jnp.transpose(kernel[:, :, :, 0, :], (0, 2, 1, 3))
     chunks, packed, left, gains = call(
         moments_kernel,
         (
@@ -445,7 +462,7 @@
         ],
         2000,
         [hbm] * 5,
-    )(*(far_memory(value) for value in (offsets, masses, table_z, table_y, gains)))
+    )(*(far_memory(value) for value in (offsets, masses, table_z, table_y, matrices)))
     chunks = lax.all_to_all(chunks, "gy", split_axis=0, concat_axis=0, tiled=True)
     lines, extended = call(
         y_forward_kernel, (shape(N * FORWARD, 128), shape(FLAT, 128)), [], 1000

time: 82 us -> 81.6 us (level)
  no operation moved by 1% of the time
where the time goes in v5:
time: 81.6 us; the launch traced here: 81.2 us
  blocking collectives  62.4 us (76%)
  Pallas kernels  9.29 us (11%)
  starting transfers between devices  7.32 us (9%)
  waiting for transfers between devices  2.16 us (3%)
    all_to_all x2, blocking collectives, exchange_rows(): rows = lax.all_to_all(rows, axis, split_axis=0, concat_axis=0, tiled=True)  47 us
    all_to_all x1, blocking collectives, stages(): lax.all_to_all(chunks, 'gy', split_axis=0, concat_axis=0, tiled=True)  15.4 us
    all_to_all x1, starting transfers between devices, stages(): lax.all_to_all(lines.reshape(8, 8, LANES), 'gy', split_axis=0, concat_axi...  7.32 us
    pallas_call x1, Pallas kernels, stages(): call(near_kernel, shape(3, 8, 512), [VMEM((3, FLAT, 128), jnp.float32)],...  3.2 us
    all_to_all x1, waiting for transfers between devices, stages(): lax.all_to_all(lines.reshape(8, 8, LANES), 'gy', split_axis=0, concat_axi...  2.16 us
    pallas_call x1, Pallas kernels, stages(): call(moments_kernel, (shape(8, 8, LANES + EDGE), shape(4, 32, 128), shape...  1.97 us
    pallas_call x1, Pallas kernels, stages(): call(spectrum_kernel, shape(N * INVERSE, 128), [VMEM((LANES, 128), jnp.fl...  1.71 us
  transfers between devices with their start and end apart: 1, of which 1 were waited for; matrix products, arithmetic and copies ran while one was open for 0% of the time, Pallas kernels for 4%

profile of v5, /device:TPU:1, one launch (start us, length us, event | category | flops | bytes accessed | tf_op | source)
XLA Modules:
  0.0 81.2 jit_solution(16607240668360002719)
XLA Ops:
  0.0 0.0 copy-start.3
  0.0 0.0 copy-start.2
  0.0 2.0 %shard_map.82 = (f32[8,8,640]{2,1,0:T(8,128)S(1)}, f32[4,32,128]{2,1,0:T(8,128)S(1)}, bf16[128,192]{1,0:T(8,128)(2,1)S(1)}, bf16[36,72,384]{2,1,0:T(8,128)(2,1)S(1)}) custom-call(f32[3,1,8,512]{3,2,1,0:T(8,128)} %offsets.1, f32[1,8,512]{2,1,0:T(8,128)} %masses_hbm.1, bf16[256,128]{1,0:T(8,128)(2,1)} %constant.10.clone.table_hbm, ...), custom_call_target="tpu_custom_call" | custom-call | flops 2000000 | bytes 2000 | tf_op jit(solution)/shard_map/pallas_call | solution.py:448
  2.0 0.0 copy-start
  2.0 0.0 copy-start.1
  2.0 15.4 %all_to_all.20.chunks = f32[8,8,640]{2,1,0:T(8,128)S(1)} all-to-all(f32[8,8,640]{2,1,0:T(8,128)S(1)} %get-tuple-element.11), channel_id=1, replica_groups=mesh['gx'=64,'gy'=8] {'gy'}, dimensions={0} | all-to-all | bytes 327680 | tf_op jit(solution)/shard_map/all_to_all | solution.py:466
  17.4 0.3 shard_map.83
  17.7 27.1 %all_to_all.21 = f32[64,1,768]{2,1,0:T(1,128)S(1)} all-to-all(f32[64,1,768]{2,1,0:T(1,128)S(1)} %bitcast.12), channel_id=1, replica_groups=mesh['gx'=64,'gy'=8] {'gx'}, dimensions={0} | all-to-all | bytes 393216 | tf_op jit(solution)/shard_map/all_to_all | solution.py:440
  44.8 0.0 copy-done.3
  44.8 0.0 copy-done.2
  44.8 1.7 %shard_map.84 = f32[512,128]{1,0:T(8,128)S(1)} custom-call(f32[384,128]{1,0:T(8,128)S(1)} %bitcast.11, bf16[36,72,384]{2,1,0:T(8,128)(2,1)S(1)} %get-tuple-element.15.gains, bf16[256,128]{1,0:T(8,128)(2,1)S(1)} %copy-done.2, bf16[64,384]{1,0:T(8,128)(2,1)S(1)} %copy-done.3), custom_call_target="tpu_custom_call" | custom-call | flops 3000000 | bytes 3000 | tf_op jit(solution)/shard_map/pallas_call | solution.py:471
  46.5 19.9 %all_to_all.22 = f32[64,8,128]{2,1,0:T(8,128)S(1)} all-to-all(f32[64,8,128]{2,1,0:T(8,128)S(1)} %bitcast.10), channel_id=1, replica_groups=mesh['gx'=64,'gy'=8] {'gx'}, dimensions={0} | all-to-all | bytes 524288 | tf_op jit(solution)/shard_map/all_to_all | solution.py:440
  66.4 0.9 %shard_map.85 = f32[64,384]{1,0:T(8,128)} custom-call(f32[512,128]{1,0:T(8,128)S(1)} %bitcast.8, bf16[128,192]{1,0:T(8,128)(2,1)S(1)} %get-tuple-element.13.table), custom_call_target="tpu_custom_call" | custom-call | flops 1000000 | bytes 1000 | tf_op jit(solution)/shard_map/pallas_call | solution.py:486
  67.4 7.3 %all-to-all-start.3 = ((f32[8,8,384]{2,1,0:T(8,128)}), f32[8,8,384]{2,1,0:T(8,128)S(1)}, u32[]{:S(2)}, u32[]{:S(2)}) async-start(f32[8,8,384]{2,1,0:T(8,128)} %bitcast.6), calls=%async_computation.3 | async-start | bytes 196608 | tf_op jit(solution)/shard_map/all_to_all | solution.py:487
  74.7 3.2 %shard_map.86.near = f32[3,8,512]{2,1,0:T(8,128)S(1)} custom-call(f32[512,128]{1,0:T(8,128)S(1)} %bitcast.9, f32[160,128]{1,0:T(8,128)S(1)} %get-tuple-element.16.own), custom_call_target="tpu_custom_call" | custom-call | flops 6000000 | bytes 6000 | tf_op jit(solution)/shard_map/pallas_call | solution.py:483
  77.9 2.2 %all-to-all-done.3.chunks = f32[8,8,384]{2,1,0:T(8,128)S(1)} async-done(((f32[8,8,384]{2,1,0:T(8,128)}), f32[8,8,384]{2,1,0:T(8,128)S(1)}, u32[]{:S(2)}, u32[]{:S(2)}) %all-to-all-start.3) | async-done | bytes 98336 | tf_op jit(solution)/shard_map/all_to_all | solution.py:487
  80.0 0.0 copy-done
  80.0 0.0 copy-done.1
  80.0 1.2 %shard_map.87 = f32[3,1,8,512]{3,2,1,0:T(8,128)} custom-call(f32[8,8,384]{2,1,0:T(8,128)S(1)} %all-to-all-done.3.chunks, f32[3,1,8,512]{3,2,1,0:T(8,128)S(1)} %copy-done, f32[3,8,512]{2,1,0:T(8,128)S(1)} %shard_map.86.near, bf16[384,128]{1,0:T(8,128)(2,1)S(1)} %copy-done.1), custom_call_target="tpu_custom_call" | custom-call | flops 2000000 | bytes 2000 | tf_op jit(solution)/shard_map/pallas_call | solution.py:490
Async XLA Ops:
  0.0 44.8 %copy-start.3 = (bf16[64,384]{1,0:T(8,128)(2,1)S(1)}, bf16[64,384]{1,0:T(8,128)(2,1)}, u32[]{:S(2)}) copy-start(bf16[64,384]{1,0:T(8,128)(2,1)} %constant.13.clone.inverse) | copy-start | bytes 147460
  0.0 44.8 %copy-start.2 = (bf16[256,128]{1,0:T(8,128)(2,1)S(1)}, bf16[256,128]{1,0:T(8,128)(2,1)}, u32[]{:S(2)}) copy-start(bf16[256,128]{1,0:T(8,128)(2,1)} %constant.12.clone.forward) | copy-start | bytes 196612
  2.0 78.0 %copy-start = (f32[3,1,8,512]{3,2,1,0:T(8,128)S(1)}, f32[3,1,8,512]{3,2,1,0:T(8,128)}, u32[]{:S(2)}) copy-start(f32[3,1,8,512]{3,2,1,0:T(8,128)} %offsets.1) | copy-start | bytes 147460
  2.0 78.0 %copy-start.1 = (bf16[384,128]{1,0:T(8,128)(2,1)S(1)}, bf16[384,128]{1,0:T(8,128)(2,1)}, u32[]{:S(2)}) copy-start(bf16[384,128]{1,0:T(8,128)(2,1)} %constant.14.clone.table) | copy-start | bytes 294916
  67.4 12.7 %all-to-all-start.3 = ((f32[8,8,384]{2,1,0:T(8,128)}), f32[8,8,384]{2,1,0:T(8,128)S(1)}, u32[]{:S(2)}, u32[]{:S(2)}) async-start(f32[8,8,384]{2,1,0:T(8,128)} %bitcast.6), calls=%async_computation.3 | async-start | bytes 196608 | tf_op jit(solution)/shard_map/all_to_all | solution.py:487

commit v6 on v5

--- a/solution.py
+++ b/solution.py
@@ -263,7 +263,8 @@
         spec[0, pair] = jnp.where(first_half, real_first[2 * pair], imag_first[2 * pair + 1])
         spec[1, pair] = jnp.where(first_half, imag_first[2 * pair], real_first[2 * pair + 1])
 
-    coeff[...] = jnp.zeros_like(coeff)
+    used = MOMENTS * GROUP
+    coeff[used:, :] = jnp.zeros((LANES - used, 128), jnp.float32)
     for pair in range(3):
         where = slice(128 * pair, 128 * pair + 128)
 
@@ -275,7 +276,7 @@
             return by_real, by_imag
 
         zero = jnp.zeros((2 * MOMENTS, 128), jnp.float32)
-        sums[0], sums[1] = lax.fori_loop(0, MOMENTS, add_channel, (zero, zero), unroll=4)
+        sums[0], sums[1] = lax.fori_loop(0, MOMENTS, add_channel, (zero, zero), unroll=MOMENTS)
         even, odd = pl.ds(0, MOMENTS, stride=2), pl.ds(1, MOMENTS, stride=2)
         real_part = sums[0, even, :] - sums[1, odd, :]
         imag_part = sums[0, odd, :] + sums[1, even, :]

time: 81.6 us -> 81.3 us (level)
  no operation moved by 1% of the time
where the time goes in v6:
time: 81.3 us; the launch traced here: 81 us
  blocking collectives  62.4 us (77%)
  Pallas kernels  9.01 us (11%)
  starting transfers between devices  7.32 us (9%)
  waiting for transfers between devices  2.16 us (3%)
    all_to_all x2, blocking collectives, exchange_rows(): rows = lax.all_to_all(rows, axis, split_axis=0, concat_axis=0, tiled=True)  47 us
    all_to_all x1, blocking collectives, stages(): lax.all_to_all(chunks, 'gy', split_axis=0, concat_axis=0, tiled=True)  15.4 us
    all_to_all x1, starting transfers between devices, stages(): lax.all_to_all(lines.reshape(8, 8, LANES), 'gy', split_axis=0, concat_axi...  7.32 us
    pallas_call x1, Pallas kernels, stages(): call(near_kernel, shape(3, 8, 512), [VMEM((3, FLAT, 128), jnp.float32)],...  3.2 us
    all_to_all x1, waiting for transfers between devices, stages(): lax.all_to_all(lines.reshape(8, 8, LANES), 'gy', split_axis=0, concat_axi...  2.16 us
    pallas_call x1, Pallas kernels, stages(): call(moments_kernel, (shape(8, 8, LANES + EDGE), shape(4, 32, 128), shape...  1.97 us
  transfers between devices with their start and end apart: 1, of which 1 were waited for; matrix products, arithmetic and copies ran while one was open for 0% of the time, Pallas kernels for 4%

profile of v6, /device:TPU:1, one launch (start us, length us, event | category | flops | bytes accessed | tf_op | source)
XLA Modules:
  0.0 81.0 jit_solution(10245362423328186872)
XLA Ops:
  0.0 0.0 copy-start.3
  0.0 0.0 copy-start.2
  0.0 2.0 %shard_map.82 = (f32[8,8,640]{2,1,0:T(8,128)S(1)}, f32[4,32,128]{2,1,0:T(8,128)S(1)}, bf16[128,192]{1,0:T(8,128)(2,1)S(1)}, bf16[36,72,384]{2,1,0:T(8,128)(2,1)S(1)}) custom-call(f32[3,1,8,512]{3,2,1,0:T(8,128)} %offsets.1, f32[1,8,512]{2,1,0:T(8,128)} %masses_hbm.1, bf16[256,128]{1,0:T(8,128)(2,1)} %constant.10.clone.table_hbm, ...), custom_call_target="tpu_custom_call" | custom-call | flops 2000000 | bytes 2000 | tf_op jit(solution)/shard_map/pallas_call | solution.py:449
  2.0 0.0 copy-start
  2.0 0.0 copy-start.1
  2.0 15.4 %all_to_all.20.chunks = f32[8,8,640]{2,1,0:T(8,128)S(1)} all-to-all(f32[8,8,640]{2,1,0:T(8,128)S(1)} %get-tuple-element.11), channel_id=1, replica_groups=mesh['gx'=64,'gy'=8] {'gy'}, dimensions={0} | all-to-all | bytes 327680 | tf_op jit(solution)/shard_map/all_to_all | solution.py:467
  17.4 0.3 shard_map.83
  17.7 27.1 %all_to_all.21 = f32[64,1,768]{2,1,0:T(1,128)S(1)} all-to-all(f32[64,1,768]{2,1,0:T(1,128)S(1)} %bitcast.12), channel_id=1, replica_groups=mesh['gx'=64,'gy'=8] {'gx'}, dimensions={0} | all-to-all | bytes 393216 | tf_op jit(solution)/shard_map/all_to_all | solution.py:441
  44.8 0.0 copy-done.3
  44.8 0.0 copy-done.2
  44.8 1.4 %shard_map.84 = f32[512,128]{1,0:T(8,128)S(1)} custom-call(f32[384,128]{1,0:T(8,128)S(1)} %bitcast.11, bf16[36,72,384]{2,1,0:T(8,128)(2,1)S(1)} %get-tuple-element.15.gains, bf16[256,128]{1,0:T(8,128)(2,1)S(1)} %copy-done.2, bf16[64,384]{1,0:T(8,128)(2,1)S(1)} %copy-done.3), custom_call_target="tpu_custom_call" | custom-call | flops 3000000 | bytes 3000 | tf_op jit(solution)/shard_map/pallas_call | solution.py:472
  46.3 19.9 %all_to_all.22 = f32[64,8,128]{2,1,0:T(8,128)S(1)} all-to-all(f32[64,8,128]{2,1,0:T(8,128)S(1)} %bitcast.10), channel_id=1, replica_groups=mesh['gx'=64,'gy'=8] {'gx'}, dimensions={0} | all-to-all | bytes 524288 | tf_op jit(solution)/shard_map/all_to_all | solution.py:441
  66.1 0.9 %shard_map.85 = f32[64,384]{1,0:T(8,128)} custom-call(f32[512,128]{1,0:T(8,128)S(1)} %bitcast.8, bf16[128,192]{1,0:T(8,128)(2,1)S(1)} %get-tuple-element.13.table), custom_call_target="tpu_custom_call" | custom-call | flops 1000000 | bytes 1000 | tf_op jit(solution)/shard_map/pallas_call | solution.py:487
  67.1 7.3 %all-to-all-start.3 = ((f32[8,8,384]{2,1,0:T(8,128)}), f32[8,8,384]{2,1,0:T(8,128)S(1)}, u32[]{:S(2)}, u32[]{:S(2)}) async-start(f32[8,8,384]{2,1,0:T(8,128)} %bitcast.6), calls=%async_computation.3 | async-start | bytes 196608 | tf_op jit(solution)/shard_map/all_to_all | solution.py:488
  74.4 3.2 %shard_map.86.near = f32[3,8,512]{2,1,0:T(8,128)S(1)} custom-call(f32[512,128]{1,0:T(8,128)S(1)} %bitcast.9, f32[160,128]{1,0:T(8,128)S(1)} %get-tuple-element.16.own), custom_call_target="tpu_custom_call" | custom-call | flops 6000000 | bytes 6000 | tf_op jit(solution)/shard_map/pallas_call | solution.py:484
  77.6 2.2 %all-to-all-done.3.chunks = f32[8,8,384]{2,1,0:T(8,128)S(1)} async-done(((f32[8,8,384]{2,1,0:T(8,128)}), f32[8,8,384]{2,1,0:T(8,128)S(1)}, u32[]{:S(2)}, u32[]{:S(2)}) %all-to-all-start.3) | async-done | bytes 98336 | tf_op jit(solution)/shard_map/all_to_all | solution.py:488
  79.8 0.0 copy-done
  79.8 0.0 copy-done.1
  79.8 1.2 %shard_map.87 = f32[3,1,8,512]{3,2,1,0:T(8,128)} custom-call(f32[8,8,384]{2,1,0:T(8,128)S(1)} %all-to-all-done.3.chunks, f32[3,1,8,512]{3,2,1,0:T(8,128)S(1)} %copy-done, f32[3,8,512]{2,1,0:T(8,128)S(1)} %shard_map.86.near, bf16[384,128]{1,0:T(8,128)(2,1)S(1)} %copy-done.1), custom_call_target="tpu_custom_call" | custom-call | flops 2000000 | bytes 2000 | tf_op jit(solution)/shard_map/pallas_call | solution.py:491
Async XLA Ops:
  0.0 44.8 %copy-start.3 = (bf16[64,384]{1,0:T(8,128)(2,1)S(1)}, bf16[64,384]{1,0:T(8,128)(2,1)}, u32[]{:S(2)}) copy-start(bf16[64,384]{1,0:T(8,128)(2,1)} %constant.13.clone.inverse) | copy-start | bytes 147460
  0.0 44.8 %copy-start.2 = (bf16[256,128]{1,0:T(8,128)(2,1)S(1)}, bf16[256,128]{1,0:T(8,128)(2,1)}, u32[]{:S(2)}) copy-start(bf16[256,128]{1,0:T(8,128)(2,1)} %constant.12.clone.forward) | copy-start | bytes 196612
  2.0 77.8 %copy-start = (f32[3,1,8,512]{3,2,1,0:T(8,128)S(1)}, f32[3,1,8,512]{3,2,1,0:T(8,128)}, u32[]{:S(2)}) copy-start(f32[3,1,8,512]{3,2,1,0:T(8,128)} %offsets.1) | copy-start | bytes 147460
  2.0 77.8 %copy-start.1 = (bf16[384,128]{1,0:T(8,128)(2,1)S(1)}, bf16[384,128]{1,0:T(8,128)(2,1)}, u32[]{:S(2)}) copy-start(bf16[384,128]{1,0:T(8,128)(2,1)} %constant.14.clone.table) | copy-start | bytes 294916
  67.1 12.7 %all-to-all-start.3 = ((f32[8,8,384]{2,1,0:T(8,128)}), f32[8,8,384]{2,1,0:T(8,128)S(1)}, u32[]{:S(2)}, u32[]{:S(2)}) async-start(f32[8,8,384]{2,1,0:T(8,128)} %bitcast.6), calls=%async_computation.3 | async-start | bytes 196608 | tf_op jit(solution)/shard_map/all_to_all | solution.py:488
